TPU v7x, 128 devices: a whole 4x4x4 slice. The times are simulated.
128 devices in a mesh: ctx: 16 (over x, y_lo, core), head: 8 (over z, y_hi).
Axes of the slice: x: 4, y: 4 (y_hi: 2, y_lo: 2; y = y_hi * 2 + y_lo), z: 4, core: 2. Of those that a mesh axis runs over, the one named last changes fastest.
Arguments:
- queries: bfloat16 [4096, 8192], P(('ctx', 'head')), may hold values from -6 to 6
- key_rows: bfloat16 [4096, 1024], P(('ctx', 'head')), may hold values from -6 to 6
- value_rows: bfloat16 [4096, 1024], P(('ctx', 'head')), may hold values from -6 to 6
- cotangent: bfloat16 [4096, 8192], P(('ctx', 'head')), may hold values from -6 to 6
- doc_lengths: int32 [8], replicated, may hold values from 1 to 2048, 4096 in all
- block_route: int32 [16, 16], replicated, may hold values from 0 to 15, each once within a row
Outputs:
- attended: bfloat16 [4096, 8192], P('ctx', 'head')
- grad_query: float32 [4096, 8192], P('ctx', 'head')
- grad_key: float32 [4096, 1024], P('ctx', 'head')
- grad_value: float32 [4096, 1024], P('ctx', 'head')
Inputs may be any that keep to these rules, and one draw needn't show every extreme that they name: `doc_lengths`: the lengths split the 4096 positions into consecutive documents; the longest is exactly 2048. Each row is a permutation: block b (16 positions) of loader shard s goes to context shard block_route[s, b].
All inputs are finite; a program needn't handle non-finite values.
Results may differ from a plain program's by a relative error of at most 0.028.
Values may be sent and summed in bfloat16 or wider, within the bound.
A program may use at most 64 MiB of HBM per device.

v0:
```python
import math

import jax
import jax.numpy as jnp
from jax import lax
from jax.sharding import PartitionSpec as P

HD = 128


NEGATIVE = -1e30


def slot_positions(block_route, shard_count, shard_rows):
    block_rows = shard_rows // shard_count
    slots = jnp.arange(shard_count * shard_rows, dtype=jnp.int32)
    target = slots // shard_rows
    source = slots % shard_rows // block_rows
    within = slots % block_rows
    blocks = jnp.arange(shard_count, dtype=jnp.int32)
    block_of = jnp.sum(
        jnp.where(block_route[:, :, None] == blocks[None, None, :], blocks[None, :, None], 0),
        axis=1,
    )
    chosen = jnp.take(block_of.reshape(-1), source * shard_count + target)
    return source * shard_rows + chosen * block_rows + within


def tile_split(count, limit):
    width = math.gcd(count, limit)
    return (count // width, width)


def on_device(queries, key_rows, value_rows, cotangent, doc_lengths, block_route):
    shard_count = lax.axis_size("ctx")
    regrouped = (
        lax.all_to_all(queries, "head", split_axis=1, concat_axis=0, tiled=True),
        lax.all_to_all(key_rows, "head", split_axis=1, concat_axis=0, tiled=True),
        lax.all_to_all(value_rows, "head", split_axis=1, concat_axis=0, tiled=True),
        lax.all_to_all(cotangent, "head", split_axis=1, concat_axis=0, tiled=True),
    )
    shard_rows = regrouped[0].shape[0]
    block_rows = shard_rows // shard_count
    own_shard = lax.axis_index("ctx")
    own_route = lax.dynamic_index_in_dim(block_route, own_shard, 0, keepdims=False)
    blocks = jnp.arange(shard_count, dtype=jnp.int32)
    outgoing = jnp.sum(jnp.where(own_route[:, None] == blocks[None, :], blocks[:, None], 0), axis=0)

    def by_target(array):
        stacked = array.reshape(shard_count, block_rows, array.shape[1])
        return jnp.take(stacked, outgoing, axis=0).reshape(shard_rows, array.shape[1])

    q_local, k_local, v_local, g_local = (
        lax.all_to_all(by_target(regrouped[0]), "ctx", split_axis=0, concat_axis=0, tiled=True),
        lax.all_to_all(by_target(regrouped[1]), "ctx", split_axis=0, concat_axis=0, tiled=True),
        lax.all_to_all(by_target(regrouped[2]), "ctx", split_axis=0, concat_axis=0, tiled=True),
        lax.all_to_all(by_target(regrouped[3]), "ctx", split_axis=0, concat_axis=0, tiled=True),
    )
    kv_heads = k_local.shape[1] // HD
    group = q_local.shape[1] // (kv_heads * HD)
    scale = 1.0 / math.sqrt(HD)
    positions = slot_positions(block_route, shard_count, shard_rows)
    ends = jnp.cumsum(doc_lengths)
    documents = jnp.sum((positions[:, None] >= ends[None, :]).astype(jnp.int32), axis=1)
    row_start = own_shard * shard_rows
    q_pos = lax.dynamic_slice_in_dim(positions, row_start, shard_rows)
    q_doc = lax.dynamic_slice_in_dim(documents, row_start, shard_rows)
    q_heads = q_local.reshape(shard_rows, kv_heads, group, HD)
    g_heads = g_local.reshape(shard_rows, kv_heads, group, HD)
    key_limit = 512

    def visibility(start, width):
        k_pos = lax.dynamic_slice_in_dim(positions, start, width)
        k_doc = lax.dynamic_slice_in_dim(documents, start, width)
        return (q_doc[:, None] == k_doc[None, :]) & (k_pos[None, :] <= q_pos[:, None])

    def over_rows(state, visible, update):
        return update(state, 0, shard_rows, visible)

    def scan_keys(state, arrays, tile_fn):
        count = arrays[0].shape[0]
        tiles, width = tile_split(count, key_limit)
        starts = jnp.arange(tiles, dtype=jnp.int32) * width

        def scan_step(carried, inputs):
            return (tile_fn(carried, inputs[:-1], inputs[-1], width), None)

        shaped = tuple((array.reshape(tiles, width, -1) for array in arrays))
        return lax.scan(scan_step, state, shaped + (starts,))[0]

    def norm_tile(state, tiles_in, start, width):
        visible = visibility(start, width)
        k_group = tiles_in[0].reshape(width, kv_heads, HD)

        def update(carried, first, last, sub_visible):
            peak, total = carried
            scores = (
                jnp.einsum("rkgd,ckd->kgrc", q_heads, k_group, preferred_element_type=jnp.float32)
                * scale
            )
            masked = jnp.where(sub_visible, scores, NEGATIVE)
            new_peak = jnp.maximum(peak, jnp.max(masked, axis=3))
            weights = jnp.where(sub_visible, jnp.exp(masked - new_peak[..., None]), 0.0)
            total = total * jnp.exp(peak - new_peak) + jnp.sum(weights, axis=3)
            return (new_peak, total)

        return over_rows(state, visible, update)

    stats_start = (
        jnp.full((kv_heads, group, shard_rows), NEGATIVE, jnp.float32),
        jnp.zeros((kv_heads, group, shard_rows), jnp.float32),
    )
    peak, total = scan_keys(
        stats_start, (lax.all_gather(k_local, "ctx", axis=0, tiled=True),), norm_tile
    )
    log_total = peak + jnp.log(total)

    def value_tile(state, tiles_in, start, width):
        visible = visibility(start, width)
        k_group = tiles_in[0].reshape(width, kv_heads, HD)
        v_group = tiles_in[1].reshape(width, kv_heads, HD)

        def update(carried, first, last, sub_visible):
            scores = (
                jnp.einsum("rkgd,ckd->kgrc", q_heads, k_group, preferred_element_type=jnp.float32)
                * scale
            )
            masked = jnp.where(sub_visible, scores, NEGATIVE)
            weights = jnp.where(sub_visible, jnp.exp(masked - log_total[..., None]), 0.0)
            return carried + jnp.einsum(
                "kgrc,ckd->kgrd",
                weights.astype(jnp.bfloat16),
                v_group,
                preferred_element_type=jnp.float32,
            )

        return over_rows(state, visible, update)

    summed = scan_keys(
        jnp.zeros((kv_heads, group, shard_rows, HD), jnp.float32),
        (
            lax.all_gather(k_local, "ctx", axis=0, tiled=True),
            lax.all_gather(v_local, "ctx", axis=0, tiled=True),
        ),
        value_tile,
    )
    attended_heads = summed.astype(jnp.bfloat16)
    attended_rows = jnp.transpose(attended_heads, (2, 0, 1, 3))
    attended = attended_rows.reshape(shard_rows, kv_heads * group * HD)
    delta = jnp.transpose(
        jnp.sum(g_heads.astype(jnp.float32) * attended_rows.astype(jnp.float32), axis=3), (1, 2, 0)
    )

    def back_block(q_block, g_block, lse_block, delta_block, visible, k_group, v_group):
        width = k_group.shape[0]
        scores = (
            jnp.einsum("rkgd,ckd->kgrc", q_block, k_group, preferred_element_type=jnp.float32)
            * scale
        )
        masked = jnp.where(visible, scores, NEGATIVE)
        weights = jnp.where(visible, jnp.exp(masked - lse_block[..., None]), 0.0)
        dprob = jnp.einsum("rkgd,ckd->kgrc", g_block, v_group, preferred_element_type=jnp.float32)
        dscore = (weights * (dprob - delta_block[..., None])).astype(jnp.bfloat16)
        added = jnp.einsum("kgrc,ckd->kgrd", dscore, k_group, preferred_element_type=jnp.float32)
        grad_k = jnp.einsum(
            "kgrc,rkgd->ckd", dscore, q_block, preferred_element_type=jnp.float32
        ).reshape(width, kv_heads * HD)
        grad_v = jnp.einsum(
            "kgrc,rkgd->ckd",
            weights.astype(jnp.bfloat16),
            g_block,
            preferred_element_type=jnp.float32,
        ).reshape(width, kv_heads * HD)
        return (added, grad_k, grad_v)

    def backward_tile(grad_q, k_tile, v_tile, start):
        width = k_tile.shape[0]
        visible = visibility(start, width)
        k_group = k_tile.reshape(width, kv_heads, HD)
        v_group = v_tile.reshape(width, kv_heads, HD)
        added, grad_k, grad_v = back_block(
            q_heads, g_heads, log_total, delta, visible, k_group, v_group
        )
        return (grad_q + added, grad_k, grad_v)

    grad_start = jnp.zeros((kv_heads, group, shard_rows, HD), jnp.float32)
    piece = (
        lax.all_gather(k_local, "ctx", axis=0, tiled=True),
        lax.all_gather(v_local, "ctx", axis=0, tiled=True),
    )
    grad_q = grad_start
    count = piece[0].shape[0]
    backward_grad_q = grad_q
    k_piece = piece[0]
    count = k_piece.shape[0]
    tiles, width = tile_split(count, key_limit)
    starts = jnp.arange(tiles, dtype=jnp.int32) * width

    def backward_step(carried, inputs):
        carried, grad_k, grad_v = backward_tile(carried, inputs[0], inputs[1], inputs[2])
        return (carried, (grad_k, grad_v))

    backward_grad_q, outputs = lax.scan(
        backward_step,
        backward_grad_q,
        (k_piece.reshape(tiles, width, -1), piece[1].reshape(tiles, width, -1), starts),
    )
    grad_q = backward_grad_q
    grad_k = outputs[0].reshape(count, kv_heads * HD)
    grad_v = outputs[1].reshape(count, kv_heads * HD)
    full_key = grad_k
    full_value = grad_v
    grad_q, full_key, full_value = (grad_q, full_key, full_value)
    key_grad, value_grad = (
        lax.psum_scatter(full_key, "ctx", scatter_dimension=0, tiled=True),
        lax.psum_scatter(full_value, "ctx", scatter_dimension=0, tiled=True),
    )
    grad_query = jnp.transpose(grad_q * scale, (2, 0, 1, 3)).reshape(
        shard_rows, kv_heads * group * HD
    )
    return (attended, grad_query, key_grad * scale, value_grad)


def solution(mesh):
    placed = (
        P(("ctx", "head"), None),
        P(("ctx", "head"), None),
        P(("ctx", "head"), None),
        P(("ctx", "head"), None),
        P(),
        P(),
    )
    return jax.shard_map(
        on_device,
        mesh=mesh,
        in_specs=placed,
        out_specs=(P("ctx", "head"), P("ctx", "head"), P("ctx", "head"), P("ctx", "head")),
        check_vma=False,
    )
```

profile of v0, /device:TPU:1, one launch (start us, length us, event | category | flops | bytes accessed | tf_op | source)
XLA Modules:
  0.0 509.6 jit_solution(5879755267113189933)
XLA Ops:
  8.7 8.5 %all-to-all-start = ((bf16[32,8,128]{2,0,1:T(8,128)(2,1)}), bf16[32,8,128]{2,0,1:T(8,128)(2,1)S(1)}, u32[]{:S(2)}, u32[]{:S(2)}) async-start(bf16[32,8,128]{2,0,1:T(8,128)(2,1)} %copy_bitcast_fusion.5), calls=%async_computation | async-start | bytes 131072 | tf_op jit(solution)/shard_map/all_to_all | solution.py:38
  19.4 4.4 all-to-all-done
  23.8 3.4 all-to-all-start.4
  27.8 6.0 %all-to-all-done.4 = bf16[32,8,128]{2,0,1:T(8,128)(2,1)S(1)} async-done(((bf16[32,8,128]{2,0,1:T(8,128)(2,1)}), bf16[32,8,128]{2,0,1:T(8,128)(2,1)S(1)}, u32[]{:S(2)}, u32[]{:S(2)}) %all-to-all-start.4) | async-done | bytes 65568 | tf_op jit(solution)/shard_map/all_to_all | solution.py:39
  35.1 7.7 %all-to-all-start.1 = ((bf16[16,16,128]{2,1,0:T(8,128)(2,1)}), bf16[16,16,128]{2,1,0:T(8,128)(2,1)S(1)}, u32[]{:S(2)}, u32[]{:S(2)}) async-start(bf16[16,16,128]{2,1,0:T(8,128)(2,1)} %get-tuple-element.539), calls=%async_computation.1 | async-start | bytes 131072 | tf_op jit(solution)/shard_map/all_to_all | solution.py:55
  44.7 4.0 all-to-all-done.1
  48.7 3.5 all-to-all-start.6
  54.1 9.0 %all-to-all-done.6 = bf16[32,8,1024]{2,0,1:T(8,128)(2,1)S(1)} async-done(((bf16[32,8,1024]{2,0,1:T(8,128)(2,1)}), bf16[32,8,1024]{2,0,1:T(8,128)(2,1)S(1)}, u32[]{:S(2)}, u32[]{:S(2)}) %all-to-all-start.6) | async-done | bytes 524320 | tf_op jit(solution)/shard_map/all_to_all | solution.py:40
  63.1 3.5 all-to-all-start.2
  67.9 8.5 %all-to-all-done.2 = bf16[32,8,1024]{2,0,1:T(8,128)(2,1)S(1)} async-done(((bf16[32,8,1024]{2,0,1:T(8,128)(2,1)}), bf16[32,8,1024]{2,0,1:T(8,128)(2,1)S(1)}, u32[]{:S(2)}, u32[]{:S(2)}) %all-to-all-start.2) | async-done | bytes 524320 | tf_op jit(solution)/shard_map/all_to_all | solution.py:37
  76.4 6.0 %all-to-all-start.5 = ((bf16[16,16,128]{2,1,0:T(8,128)(2,1)}), bf16[16,16,128]{2,1,0:T(8,128)(2,1)S(1)}, u32[]{:S(2)}, u32[]{:S(2)}) async-start(bf16[16,16,128]{2,1,0:T(8,128)(2,1)} %get-tuple-element.538), calls=%async_computation.5 | async-start | bytes 131072 | tf_op jit(solution)/shard_map/all_to_all | solution.py:56
  84.1 4.3 all-to-all-done.5
  88.4 3.7 all-to-all-start.3
  92.2 10.1 %all-to-all-done.3 = bf16[16,16,1024]{2,1,0:T(8,128)(2,1)S(1)} async-done(((bf16[16,16,1024]{2,1,0:T(8,128)(2,1)}), bf16[16,16,1024]{2,1,0:T(8,128)(2,1)S(1)}, u32[]{:S(2)}, u32[]{:S(2)}) %all-to-all-start.3) | async-done | bytes 524320 | tf_op jit(solution)/shard_map/all_to_all | solution.py:54
  102.3 4.1 all-to-all-start.7
  106.9 25.7 %gather_fusion = s32[4096]{0:T(1024)S(1)} fusion(s32[256]{0:T(256)S(1)} %reshape.369, s32[4096]{0:T(1024)S(1)} %broadcast_clamp_fusion), kind=kCustom, calls=%fused_computation.4 | custom fusion | bytes 49152 | tf_op jit(solution)/shard_map/jit(_take)/gather | solution.py:25
  134.4 78.3 %while.39 = (s32[]{:T(128)}, f32[1,8,256]{2,1,0:T(8,128)S(1)}, f32[1,8,256]{2,1,0:T(8,128)S(1)}, s32[256]{0:T(256)S(1)}, s32[8]{0:T(128)S(1)}, /*index=5*/s32[40...) while((s32[]{:T(128)}, f32[1,8,256]{2,1,0:T(8,128)S(1)}, ...), condition=%wide.region_7.10_spmd.clone, body=%wide.region_4.9_spmd.clone.sunk | while | flops 277227520 | bytes 9558718 | solution.py:89
  137.3 3.6 fusion.117
  141.0 3.2 select_reduce_fusion.4
  147.1 3.6 fusion.117
  150.8 3.2 select_reduce_fusion.4
  156.9 3.6 fusion.117
  160.6 3.2 select_reduce_fusion.4
  166.7 3.6 fusion.117
  170.3 3.2 select_reduce_fusion.4
  176.5 3.6 fusion.117
  180.1 3.2 select_reduce_fusion.4
  186.3 3.6 fusion.117
  189.9 3.2 select_reduce_fusion.4
  196.0 3.6 fusion.117
  199.7 3.2 select_reduce_fusion.4
  205.8 3.7 fusion.117
  209.5 3.2 select_reduce_fusion.4
  212.7 47.9 %while.40 = (s32[]{:T(128)}, f32[1,8,256,128]{3,2,1,0:T(8,128)S(1)}, s32[256]{0:T(256)S(1)}, s32[8]{0:T(128)S(1)}, s32[4096]{0:T(1024)S(1)}, /*index=5*/s32[4096...) while((s32[]{:T(128)}, ...), condition=%wide.region_9.12_spmd.clone, body=%wide.region_8.11_spmd.clone.sunk | while | flops 543031296 | bytes 3169477 | solution.py:89
  215.7 3.1 fusion.122
  221.7 3.1 fusion.122
  227.6 3.1 fusion.122
  233.6 3.1 fusion.122
  239.6 3.1 fusion.122
  245.6 3.1 fusion.122
  251.6 3.1 fusion.122
  257.6 3.1 fusion.122
  261.5 116.3 %while.41 = (s32[]{:T(128)}, f32[1,8,256,128]{3,2,1,0:T(8,128)}, f32[8,512,128]{2,1,0:T(8,128)}, f32[8,512,128]{2,1,0:T(8,128)}, s32[256]{0:T(256)S(1)}, /*index...) while((s32[]{:T(128)}, f32[1,8,256,128]{3,2,1,0:T(8,128)}, ...), condition=%wide.region_12.15_spmd.clone, body=%wide.region_11.14_spmd.clone.sunk | while | flops 1355677696 | bytes 60072760 | solution.py:203
  266.1 2.6 fusion.134
  270.1 2.8 fusion.135
  272.8 2.9 fusion.137
  284.2 3.2 fusion.135
  287.4 2.9 fusion.137
  294.8 2.6 fusion.134
  298.8 3.2 fusion.135
  302.0 2.9 fusion.137
  313.4 3.2 fusion.135
  316.6 2.9 fusion.137
  328.0 3.2 fusion.135
  331.2 2.9 fusion.137
  342.6 3.2 fusion.135
  345.8 2.9 fusion.137
  357.2 3.2 fusion.135
  360.3 2.9 fusion.137
  367.8 2.6 fusion.134
  371.8 3.2 fusion.135
  374.9 2.9 fusion.137
  381.8 55.2 %reduce-scatter.3.cloned.1.call-done = f32[256,128]{1,0:T(8,128)} async-done(((f32[4096,128]{1,0:T(8,128)}), f32[256,128]{1,0:T(8,128)}) %reduce-scatter.3.cloned.1.call-update) | async-done | bytes 131088 | tf_op jit(solution)/shard_map/reduce_scatter | solution.py:215
  438.6 64.4 %reduce-scatter.5.cloned.1.call-done = f32[256,128]{1,0:T(8,128)} async-done(((f32[4096,128]{1,0:T(8,128)}), f32[256,128]{1,0:T(8,128)}) %reduce-scatter.5.cloned.1.call-update) | async-done | bytes 131088 | tf_op jit(solution)/shard_map/reduce_scatter | solution.py:216
  (255 shorter events, 81.1 us)
Async XLA Ops:
  7.2 0.8 copy-start
  8.7 15.2 %all-to-all-start = ((bf16[32,8,128]{2,0,1:T(8,128)(2,1)}), bf16[32,8,128]{2,0,1:T(8,128)(2,1)S(1)}, u32[]{:S(2)}, u32[]{:S(2)}) async-start(bf16[32,8,128]{2,0,1:T(8,128)(2,1)} %copy_bitcast_fusion.5), calls=%async_computation | async-start | bytes 131072 | tf_op jit(solution)/shard_map/all_to_all | solution.py:38
  23.8 10.0 %all-to-all-start.4 = ((bf16[32,8,128]{2,0,1:T(8,128)(2,1)}), bf16[32,8,128]{2,0,1:T(8,128)(2,1)S(1)}, u32[]{:S(2)}, u32[]{:S(2)}) async-start(bf16[32,8,128]{2,0,1:T(8,128)(2,1)} %copy_bitcast_fusion.4), calls=%async_computation.4 | async-start | bytes 131072 | tf_op jit(solution)/shard_map/all_to_all | solution.py:39
  35.1 13.5 %all-to-all-start.1 = ((bf16[16,16,128]{2,1,0:T(8,128)(2,1)}), bf16[16,16,128]{2,1,0:T(8,128)(2,1)S(1)}, u32[]{:S(2)}, u32[]{:S(2)}) async-start(bf16[16,16,128]{2,1,0:T(8,128)(2,1)} %get-tuple-element.539), calls=%async_computation.1 | async-start | bytes 131072 | tf_op jit(solution)/shard_map/all_to_all | solution.py:55
  48.7 18.0 %copy-start.6 = (bf16[16,16,128]{2,1,0:T(8,128)(2,1)}, bf16[16,16,128]{2,1,0:T(8,128)(2,1)S(1)}, u32[]{:S(2)}) copy-start(bf16[16,16,128]{2,1,0:T(8,128)(2,1)S(1)} %all-to-all-done.1) | copy-start | bytes 196612
  48.7 14.4 %all-to-all-start.6 = ((bf16[32,8,1024]{2,0,1:T(8,128)(2,1)}), bf16[32,8,1024]{2,0,1:T(8,128)(2,1)S(1)}, u32[]{:S(2)}, u32[]{:S(2)}) async-start(bf16[32,8,1024]{2,0,1:T(8,128)(2,1)} %bitcast.239), calls=%async_computation.6 | async-start | bytes 1048576 | tf_op jit(solution)/shard_map/all_to_all | solution.py:40
  52.2 54.3 %copy-start.7 = (s32[16,16]{1,0:T(8,128)S(1)}, s32[16,16]{1,0:T(8,128)}, u32[]{:S(2)}) copy-start(s32[16,16]{1,0:T(8,128)} %param.21) | copy-start | bytes 3076
  52.2 54.6 %copy-start.8 = (s32[8]{0:T(128)S(1)}, s32[8]{0:T(128)}, u32[]{:S(2)}) copy-start(s32[8]{0:T(128)} %param.20) | copy-start | bytes 100
  63.1 13.3 %all-to-all-start.2 = ((bf16[32,8,1024]{2,0,1:T(8,128)(2,1)}), bf16[32,8,1024]{2,0,1:T(8,128)(2,1)S(1)}, u32[]{:S(2)}, u32[]{:S(2)}) async-start(bf16[32,8,1024]{2,0,1:T(8,128)(2,1)} %bitcast.240), calls=%async_computation.2 | async-start | bytes 1048576 | tf_op jit(solution)/shard_map/all_to_all | solution.py:37
  66.6 67.8 %all-gather.3.cloned.1.call-start = ((), (), s32[]{:S(2)}) async-start(), calls=%async_computation.10 | async-start | bytes 1114112 | tf_op jit(solution)/shard_map/all_gather | solution.py:142
  76.4 12.0 %all-to-all-start.5 = ((bf16[16,16,128]{2,1,0:T(8,128)(2,1)}), bf16[16,16,128]{2,1,0:T(8,128)(2,1)S(1)}, u32[]{:S(2)}, u32[]{:S(2)}) async-start(bf16[16,16,128]{2,1,0:T(8,128)(2,1)} %get-tuple-element.538), calls=%async_computation.5 | async-start | bytes 131072 | tf_op jit(solution)/shard_map/all_to_all | solution.py:56
  88.4 44.3 %copy-start.5 = (bf16[16,16,128]{2,1,0:T(8,128)(2,1)}, bf16[16,16,128]{2,1,0:T(8,128)(2,1)S(1)}, u32[]{:S(2)}) copy-start(bf16[16,16,128]{2,1,0:T(8,128)(2,1)S(1)} %all-to-all-done.5) | copy-start | bytes 196612
  88.4 13.9 %all-to-all-start.3 = ((bf16[16,16,1024]{2,1,0:T(8,128)(2,1)}), bf16[16,16,1024]{2,1,0:T(8,128)(2,1)S(1)}, u32[]{:S(2)}, u32[]{:S(2)}) async-start(bf16[16,16,1024]{2,1,0:T(8,128)(2,1)} %get-tuple-element.540), calls=%async_computation.3 | async-start | bytes 1048576 | tf_op jit(solution)/shard_map/all_to_all | solution.py:54
  102.3 31.1 %all-to-all-start.7 = ((bf16[16,16,1024]{2,1,0:T(8,128)(2,1)}), bf16[16,16,1024]{2,1,0:T(8,128)(2,1)S(1)}, u32[]{:S(2)}, u32[]{:S(2)}) async-start(bf16[16,16,1024]{2,1,0:T(8,128)(2,1)} %get-tuple-element.541), calls=%async_computation.7 | async-start | bytes 1048576 | tf_op jit(solution)/shard_map/all_to_all | solution.py:57
  106.4 106.3 %all-gather.5.cloned.1.call-start = ((), (), s32[]{:S(2)}) async-start(), calls=%async_computation.11 | async-start | bytes 1114112 | tf_op jit(solution)/shard_map/all_gather | solution.py:143
  133.0 304.0 %reduce-scatter.3.cloned.1.call-start = ((), (), s32[]{:S(2)}) async-start(), calls=%async_computation.12 | async-start | bytes 2228224 | tf_op jit(solution)/shard_map/reduce_scatter | solution.py:215
  264.0 2.0 copy-start.4
  266.0 2.6 copy-start.1
  270.1 2.8 copy-start.2
  278.2 2.0 copy-start.4
  280.2 2.6 copy-start.1
  284.2 3.2 copy-start.2
  292.8 2.0 copy-start.4
  294.8 2.6 copy-start.1
  298.8 3.2 copy-start.2
  307.4 2.0 copy-start.4
  309.4 2.6 copy-start.1
  313.4 3.2 copy-start.2
  322.0 2.0 copy-start.4
  324.0 2.6 copy-start.1
  328.0 3.2 copy-start.2
  336.6 2.0 copy-start.4
  338.6 2.6 copy-start.1
  342.6 3.2 copy-start.2
  351.1 2.0 copy-start.4
  353.1 2.6 copy-start.1
  357.2 3.2 copy-start.2
  365.8 2.0 copy-start.4
  367.8 2.6 copy-start.1
  371.8 3.2 copy-start.2
  377.8 1.2 copy-start.3
  377.9 125.2 %reduce-scatter.5.cloned.1.call-start = ((), (), s32[]{:S(2)}) async-start(), calls=%async_computation.13 | async-start | bytes 2228224 | tf_op jit(solution)/shard_map/reduce_scatter | solution.py:216
Sparse Core Ops, SparseCore 0:
  69.7 34.8 all-gather.2
  133.1 30.4 all-gather.4
  378.0 59.0 reduce-scatter.2
  439.9 63.1 reduce-scatter.4
where the time goes:
time: 515 us; the launch traced here: 510 us
  waiting for transfers between devices  167 us (32%)
  matrix products  146 us (28%)
  local copies, waits for them, and re-layouts  58.1 us (11%)
  loops' own time  47.7 us (9%)
  starting transfers between devices  40.7 us (8%)
  other arithmetic  35.5 us (7%)
  between operations  14 us (3%)
    reduce_scatter x1, waiting for transfers between devices, on_device(): lax.psum_scatter(full_value, 'ctx', scatter_dimension=0, tiled=True)  64.4 us
    reduce_scatter x1, waiting for transfers between devices, on_device(): lax.psum_scatter(full_key, 'ctx', scatter_dimension=0, tiled=True)  55.2 us
    another operation x2, loops' own time, scan_keys(): return lax.scan(scan_step, state, shaped + (starts,))[0]  31.7 us
    dot_general x8, matrix products, update(): jnp.einsum('rkgd,ckd->kgrc', q_heads, k_group, preferred_element_type=jnp...  29.2 us
    gather x1, local copies, waits for them, and re-layouts, slot_positions(): chosen = jnp.take(block_of.reshape(-1), source * shard_count + target)  25.7 us
    reduce_sum x8, other arithmetic, update(): total = total * jnp.exp(peak - new_peak) + jnp.sum(weights, axis=3)  25.5 us
    dot_general x8, matrix products, back_block(): jnp.einsum('kgrc,ckd->kgrd', dscore, k_group, preferred_element_type=jnp....  24.9 us
    dot_general x8, matrix products, update(): jnp.einsum('kgrc,ckd->kgrd', weights.astype(jnp.bfloat16), v_group, prefe...  24.5 us
  transfers between devices with their start and end apart: 12, of which 9 were waited for; matrix products, arithmetic and copies ran while one was open for 20% of the time, Pallas kernels for 0%

commit v1 on v0

v1 whole, which is shorter than its diff:
```python
import math

import jax
import jax.numpy as jnp
from jax import lax
from jax.experimental import pallas as pl
from jax.experimental.pallas import tpu as pltpu
from jax.sharding import PartitionSpec as P

HD = 128
GROUP = 8
SHARDS = 16
BLOCK = 16
ROWS = SHARDS * BLOCK
SEQ = SHARDS * ROWS
DOCS = 8
HEADS = 8
COLS = GROUP * HD

SPAN = 4
LANES = SPAN * GROUP * BLOCK
NEGATIVE = -1e30
FLOOR = -0.5e30
SCALE = 1.0 / math.sqrt(HD)
LOG2E = 1.4426950408889634

BF = jnp.bfloat16
F32 = jnp.float32
MESH = pl.DeviceIdType.MESH
ANY = pl.BlockSpec(memory_space=pl.ANY)
VMEM = pl.BlockSpec(memory_space=pltpu.VMEM)
SMEM = pl.BlockSpec(memory_space=pltpu.SMEM)


def ctx_of(x, y, core):
    return (lax.rem(x, 4) * 2 + lax.rem(y, 2)) * 2 + lax.rem(core, 2)


def head_of(z, y):
    return lax.rem(z, 4) * 2 + lax.rem(y, 2)


def remote(src, dst, send, recv, ctx, head):
    return pltpu.make_async_remote_copy(
        src_ref=src,
        dst_ref=dst,
        send_sem=send,
        recv_sem=recv,
        device_id=(ctx, head),
        device_id_type=MESH,
    )


def exchange_kernel(
    route, q, k, v, g, qo, go, ko, vo, xq, xg, sq, sg,
    p1s, p1r, p2s, p2r, rs, rr, cs, cr, local,
):
    c = lax.axis_index("ctx")
    h = lax.axis_index("head")
    z, yh = h // 2, lax.rem(h, 2)
    x, yl, core = c // 4, lax.rem(c // 2, 2), lax.rem(c, 2)
    head_peers = [(jz, jy) for jz in range(4) for jy in range(2) if (jz, jy) != (0, 0)]
    ctx_peers = [
        (jx, jy, jc) for jx in range(4) for jy in range(2) for jc in range(2)
        if (jx, jy, jc) != (0, 0, 0)
    ]

    barrier = pltpu.get_barrier_semaphore()
    for jz, jy in head_peers:
        pl.semaphore_signal(
            barrier, inc=1, device_id=(c, head_of(z + jz, yh + jy)), device_id_type=MESH
        )
    for jx, jy, jc in ctx_peers:
        pl.semaphore_signal(
            barrier, inc=1, device_id=(ctx_of(x + jx, yl + jy, core + jc), h), device_id_type=MESH
        )
    pl.semaphore_wait(barrier, len(head_peers) + len(ctx_peers))

    sent = []

    def go_remote(copy):
        copy.start()
        sent.append(copy)
        return copy

    kv_rows = pl.ds(c * ROWS + h * 32, 32)
    p1 = [[], [], [], []]
    for jz, jy in head_peers:
        j = jz * 2 + jy
        peer = head_of(z + jz, yh + jy)
        cols = pl.ds(pl.multiple_of(peer * HD, HD), HD)
        for a, (src, dst) in enumerate(((k, ko), (v, vo))):
            p1[a].append(go_remote(remote(
                src.at[:, cols], dst.at[kv_rows], p1s.at[a, j], p1r.at[a, j], c, peer)))
    own_cols = pl.ds(pl.multiple_of(h * HD, HD), HD)
    own = [
        pltpu.make_async_copy(k.at[:, own_cols], ko.at[kv_rows], local.at[0]),
        pltpu.make_async_copy(v.at[:, own_cols], vo.at[kv_rows], local.at[1]),
    ]
    for a, (src, dst) in enumerate(((q, xq), (g, xg))):
        for jz, jy in head_peers:
            j = jz * 2 + jy
            peer = head_of(z + jz, yh + jy)
            cols = pl.ds(pl.multiple_of(peer * COLS, COLS), COLS)
            p1[2 + a].append(go_remote(remote(
                src.at[:, :, cols], dst.at[pl.ds(h * 2, 2)],
                p1s.at[2 + a, j], p1r.at[2 + a, j], c, peer)))
        cols = pl.ds(pl.multiple_of(h * COLS, COLS), COLS)
        own.append(pltpu.make_async_copy(
            src.at[:, :, cols], dst.at[pl.ds(h * 2, 2)], local.at[2 + a]))
    for copy in own:
        copy.start()

    kv = (ko, vo)

    def shard(a, dx, dy):
        return kv[a].at[pl.ds(ctx_of(x + dx, yl + dy, core) * ROWS, ROWS)]

    def ring(a, dx, dy, tx, ty):
        slot = ((dx - tx) % 4) * 2 + (dy - ty) % 2
        part = shard(a, dx, dy)
        return remote(part, part, rs.at[a, slot], rr.at[a, slot],
                      ctx_of(x + tx + 4, yl + ty + 2, core), h)

    def partner(a, dx, dy):
        slot = dx * 2 + dy
        part = shard(a, dx, dy)
        return remote(part, part, cs.at[a, slot], cr.at[a, slot], ctx_of(x, yl, core + 1), h)

    def arrived(a, dx, dy):
        slot = dx * 2 + dy
        part = shard(a, dx, dy)
        remote(part, part, rs.at[a, slot], rr.at[a, slot], c, h).wait_recv()

    for a in range(2):
        own[a].wait()
        for copy in p1[a]:
            copy.wait_recv()
    for a in range(2):
        go_remote(ring(a, 0, 0, 0, 1))
        go_remote(ring(a, 0, 0, 1, 0))
        go_remote(ring(a, 0, 0, -1, 0))
        go_remote(partner(a, 0, 0))

    def second(a, stage, send, out):
        own[2 + a].wait()
        for copy in p1[2 + a]:
            copy.wait_recv()

        def pick(d, carry):
            block = jnp.int32(0)
            for b in range(SHARDS):
                block = jnp.where(route[c, b] == d, b, block)
            send[d] = stage[block]
            return carry

        lax.fori_loop(0, SHARDS, pick, 0)
        mine = pltpu.make_async_copy(send.at[c], out.at[c], local.at[4 + a])
        mine.start()
        copies = []
        for jx, jy, jc in ctx_peers:
            j = (jx * 2 + jy) * 2 + jc
            d = ctx_of(x + jx, yl + jy, core + jc)
            copies.append(go_remote(remote(
                send.at[d], out.at[c], p2s.at[a, j], p2r.at[a, j], d, h)))
        return mine, copies

    for a in range(2):
        arrived(a, 0, 1)
        go_remote(ring(a, 0, 1, 1, 0))
        go_remote(ring(a, 0, 1, -1, 0))
        go_remote(partner(a, 0, 1))
    mine_q, p2q = second(0, xq, sq, qo)
    for dy in range(2):
        for a in range(2):
            arrived(a, 3, dy)
            if a == 0:
                go_remote(ring(a, 3, dy, 1, 0))
            go_remote(partner(a, 3, dy))
            arrived(a, 1, dy)
            if a == 1:
                go_remote(ring(a, 1, dy, -1, 0))
            go_remote(partner(a, 1, dy))
    mine_g, p2g = second(1, xg, sg, go)
    for dy in range(2):
        for a in range(2):
            arrived(a, 2, dy)
            go_remote(partner(a, 2, dy))
    mine_q.wait()
    mine_g.wait()

    def received(a, out):
        for jx, jy, jc in ctx_peers:
            j = (jx * 2 + jy) * 2 + jc
            src = ctx_of(x - jx + 4, yl - jy + 2, core - jc + 2)
            remote(out.at[src], out.at[src], p2s.at[a, j], p2r.at[a, j], c, h).wait_recv()

    received(0, qo)
    received(1, go)
    for a in range(2):
        for dx in range(4):
            for dy in range(2):
                slot = dx * 2 + dy
                part = kv[a].at[pl.ds(ctx_of(x + dx, yl + dy, core + 1) * ROWS, ROWS)]
                remote(part, part, cs.at[a, slot], cr.at[a, slot], c, h).wait_recv()
    for copy in sent:
        copy.wait_send()


def exchange(route, q, k, v, g):
    return pl.pallas_call(
        exchange_kernel,
        name="exchange",
        out_shape=(
            jax.ShapeDtypeStruct((SHARDS, BLOCK, COLS), BF),
            jax.ShapeDtypeStruct((SHARDS, BLOCK, COLS), BF),
            jax.ShapeDtypeStruct((SEQ, HD), BF),
            jax.ShapeDtypeStruct((SEQ, HD), BF),
        ),
        in_specs=[SMEM, ANY, VMEM, VMEM, ANY],
        out_specs=(ANY, ANY, ANY, ANY),
        scratch_shapes=[
            pltpu.VMEM((SHARDS, BLOCK, COLS), BF),
            pltpu.VMEM((SHARDS, BLOCK, COLS), BF),
            pltpu.VMEM((SHARDS, BLOCK, COLS), BF),
            pltpu.VMEM((SHARDS, BLOCK, COLS), BF),
            pltpu.SemaphoreType.DMA((4, 8)),
            pltpu.SemaphoreType.DMA((4, 8)),
            pltpu.SemaphoreType.DMA((2, 16)),
            pltpu.SemaphoreType.DMA((2, 16)),
            pltpu.SemaphoreType.DMA((2, 24)),
            pltpu.SemaphoreType.DMA((2, 8)),
            pltpu.SemaphoreType.DMA((2, 8)),
            pltpu.SemaphoreType.DMA((2, 8)),
            pltpu.SemaphoreType.DMA((6,)),
        ],
        compiler_params=pltpu.CompilerParams(collective_id=0, has_side_effects=True),
    )(route, q, k, v, g)


def attention_kernel(
    route, docs, q, g, k, v, att, dq, dkv,
    s_buf, kt, vt, dk_acc, dv_acc, ot_acc, dqt_acc, starts,
):
    c = lax.axis_index("ctx")
    ends = []
    total = jnp.int32(0)
    for j in range(DOCS):
        total = total + docs[j]
        ends.append(total)

    def find(s, carry):
        block = jnp.int32(0)
        for b in range(SHARDS):
            block = jnp.where(route[s, b] == c, b, block)
        starts[s] = s * ROWS + block * BLOCK
        return carry

    lax.fori_loop(0, SHARDS, find, 0)

    def prepare(t, carry):
        kt[t] = k[pl.ds(t * ROWS, ROWS), :].T
        vt[t] = v[pl.ds(t * ROWS, ROWS), :].T
        zero = jnp.zeros((ROWS, HD), F32)
        dk_acc[pl.ds(t * ROWS, ROWS), :] = zero
        dv_acc[pl.ds(t * ROWS, ROWS), :] = zero
        return carry

    lax.fori_loop(0, SHARDS, prepare, 0)

    def stack(ref, first):
        parts = []
        for i in range(SPAN):
            rows = ref[first + i]
            parts += [rows[:, n * HD:(n + 1) * HD] for n in range(GROUP)]
        return jnp.concatenate(parts, axis=0)

    lane = lax.broadcasted_iota(jnp.int32, (1, GROUP * BLOCK), 1)
    within = lax.rem(lane, BLOCK)

    def group(n, carry):
        first = n * SPAN
        qg = stack(q, first)
        gg = stack(g, first)
        qt = qg.T
        gt = gg.T
        q_pos = jnp.concatenate([within + starts[first + i] for i in range(SPAN)], axis=1)
        q_doc = jnp.zeros_like(q_pos)
        low = jnp.int32(0)
        p_first = starts[first]
        for end in ends:
            q_doc = jnp.where(q_pos >= end, end, q_doc)
            low = jnp.where(p_first >= end, end, low)
        t_low = low // ROWS
        t_high = first + SPAN
        key = lax.broadcasted_iota(jnp.int32, (ROWS, LANES), 0)
        ot_acc[...] = jnp.zeros_like(ot_acc)
        dqt_acc[...] = jnp.zeros_like(dqt_acc)

        def forward(t, carried):
            peak, mass = carried
            s = jnp.dot(k[pl.ds(t * ROWS, ROWS), :], qt, preferred_element_type=F32)
            base = t * ROWS
            seen = (key >= q_doc - base) & (key <= q_pos - base)
            s = jnp.where(seen, s * (SCALE * LOG2E), NEGATIVE)
            s_buf[t] = s
            new_peak = jnp.maximum(peak, jnp.max(s, axis=0, keepdims=True))
            p = jnp.exp2(s - new_peak)
            fade = jnp.exp2(peak - new_peak)
            mass = mass * fade + jnp.sum(p, axis=0, keepdims=True)
            ot_acc[...] = ot_acc[...] * fade + jnp.dot(
                vt[t], p.astype(BF), preferred_element_type=F32)
            return new_peak, mass

        peak, mass = lax.fori_loop(
            t_low, t_high, forward,
            (jnp.full((1, LANES), FLOOR, F32), jnp.zeros((1, LANES), F32)))
        lse = peak + jnp.log2(mass)
        ot = (ot_acc[...] * (1.0 / mass)).astype(BF)
        delta = jnp.sum(gt.astype(F32) * ot.astype(F32), axis=0, keepdims=True)
        o = ot.T
        for i in range(SPAN):
            for m in range(GROUP):
                r = (i * GROUP + m) * BLOCK
                att[first + i, :, m * HD:(m + 1) * HD] = o[r:r + BLOCK]

        def backward(t, carried):
            rows = pl.ds(t * ROWS, ROWS)
            p = jnp.exp2(s_buf[t] - lse)
            dp = jnp.dot(v[rows, :], gt, preferred_element_type=F32)
            ds = (p * (dp - delta)).astype(BF)
            dv_acc[rows, :] += jnp.dot(p.astype(BF), gg, preferred_element_type=F32)
            dk_acc[rows, :] += jnp.dot(ds, qg, preferred_element_type=F32)
            dqt_acc[...] += jnp.dot(kt[t], ds, preferred_element_type=F32)
            return carried

        lax.fori_loop(t_low, t_high, backward, 0)
        grad = dqt_acc[...].T * SCALE
        for i in range(SPAN):
            for m in range(GROUP):
                r = (i * GROUP + m) * BLOCK
                dq[first + i, :, m * HD:(m + 1) * HD] = grad[r:r + BLOCK]
        return carry

    lax.fori_loop(0, SHARDS // SPAN, group, 0)

    def regroup(s, carry):
        for b in range(SHARDS):
            d = route[s, b]
            to = lax.rem(d, 2) * 8 + d // 2
            rows = pl.ds(s * ROWS + b * BLOCK, BLOCK)
            dkv[to, 0, s] = (dk_acc[rows, :] * SCALE).astype(BF)
            dkv[to, 1, s] = dv_acc[rows, :].astype(BF)
        return carry

    lax.fori_loop(0, SHARDS, regroup, 0)


def attention(route, docs, q, g, k, v):
    return pl.pallas_call(
        attention_kernel,
        name="attention",
        out_shape=(
            jax.ShapeDtypeStruct((SHARDS, BLOCK, COLS), BF),
            jax.ShapeDtypeStruct((SHARDS, BLOCK, COLS), F32),
            jax.ShapeDtypeStruct((SHARDS, 2, SHARDS, BLOCK, HD), BF),
        ),
        in_specs=[SMEM, SMEM, VMEM, VMEM, VMEM, VMEM],
        out_specs=(VMEM, VMEM, VMEM),
        scratch_shapes=[
            pltpu.VMEM((SHARDS, ROWS, LANES), F32),
            pltpu.VMEM((SHARDS, HD, ROWS), BF),
            pltpu.VMEM((SHARDS, HD, ROWS), BF),
            pltpu.VMEM((SEQ, HD), F32),
            pltpu.VMEM((SEQ, HD), F32),
            pltpu.VMEM((HD, LANES), F32),
            pltpu.VMEM((HD, LANES), F32),
            pltpu.SMEM((SHARDS,), jnp.int32),
        ],
        compiler_params=pltpu.CompilerParams(vmem_limit_bytes=48 << 20),
    )(route, docs, q, g, k, v)


def reduce_kernel(part, dk, dv, mate, chip, total, s1, r1, s2, r2):
    c = lax.axis_index("ctx")
    h = lax.axis_index("head")
    x, yl, core = c // 4, lax.rem(c // 2, 2), lax.rem(c, 2)
    peers = [(jx, jy) for jx in range(4) for jy in range(2) if (jx, jy) != (0, 0)]
    order = peers + [(0, 0)]
    other = ctx_of(x, yl, core + 1)

    barrier = pltpu.get_barrier_semaphore()
    pl.semaphore_signal(barrier, inc=1, device_id=(other, h), device_id_type=MESH)
    for jx, jy in peers:
        pl.semaphore_signal(
            barrier, inc=1, device_id=(ctx_of(x + jx, yl + jy, core), h), device_id_type=MESH)
    pl.semaphore_wait(barrier, len(peers) + 1)

    def place(jx, jy):
        return lax.rem(x + jx, 4) * 2 + lax.rem(yl + jy, 2)

    first = []
    for jx, jy in order:
        j = jx * 2 + jy
        t = place(jx, jy)
        copy = remote(part.at[(1 - core) * 8 + t], mate.at[t], s1.at[j], r1.at[j], other, h)
        copy.start()
        first.append(copy)
    second = []
    for (jx, jy), copy in zip(order, first):
        j = jx * 2 + jy
        t = place(jx, jy)
        copy.wait_recv()
        pair = part[core * 8 + t].astype(F32) + mate[t].astype(F32)
        if (jx, jy) == (0, 0):
            total[...] = pair
        else:
            mate[t] = pair.astype(BF)
            copy = remote(mate.at[t], chip.at[j], s2.at[j], r2.at[j],
                          ctx_of(x + jx, yl + jy, core), h)
            copy.start()
            second.append(copy)
    for copy, (jx, jy) in zip(second, peers):
        copy.wait_recv()
        total[...] += chip[jx * 2 + jy].astype(F32)
    dk[...] = total[0]
    dv[...] = total[1]
    for copy in first + second:
        copy.wait_send()


def reduce(part):
    shape = (2, SHARDS, BLOCK, HD)
    return pl.pallas_call(
        reduce_kernel,
        name="reduce",
        out_shape=(
            jax.ShapeDtypeStruct((SHARDS, BLOCK, HD), F32),
            jax.ShapeDtypeStruct((SHARDS, BLOCK, HD), F32),
        ),
        in_specs=[VMEM],
        out_specs=(VMEM, VMEM),
        scratch_shapes=[
            pltpu.VMEM((8,) + shape, BF),
            pltpu.VMEM((8,) + shape, BF),
            pltpu.VMEM(shape, F32),
            pltpu.SemaphoreType.DMA((8,)),
            pltpu.SemaphoreType.DMA((8,)),
            pltpu.SemaphoreType.DMA((8,)),
            pltpu.SemaphoreType.DMA((8,)),
        ],
        compiler_params=pltpu.CompilerParams(collective_id=1, has_side_effects=True),
    )(part)


def on_device(queries, key_rows, value_rows, cotangent, doc_lengths, block_route):
    q, g, k, v = exchange(
        block_route,
        queries.reshape(2, BLOCK, HEADS * COLS),
        key_rows,
        value_rows,
        cotangent.reshape(2, BLOCK, HEADS * COLS),
    )
    att, dq, part = attention(block_route, doc_lengths, q, g, k, v)
    dk, dv = reduce(part)
    return (
        att.reshape(ROWS, COLS),
        dq.reshape(ROWS, COLS),
        dk.reshape(ROWS, HD),
        dv.reshape(ROWS, HD),
    )


def solution(mesh):
    placed = P(("ctx", "head"), None)
    return jax.shard_map(
        on_device,
        mesh=mesh,
        in_specs=(placed, placed, placed, placed, P(), P()),
        out_specs=(P("ctx", "head"),) * 4,
        check_vma=False,
    )
```

time: 515 us -> 109 us (0.21)
  waiting for transfers between devices: 167 us -> 0 us
  matrix products: 146 us -> 0 us
  Pallas kernels: 0 us -> 97.1 us
  local copies, waits for them, and re-layouts: 58.1 us -> 10.3 us
  loops' own time: 47.7 us -> 0 us
  starting transfers between devices: 40.7 us -> 0 us
  other arithmetic: 35.5 us -> 0 us
  between operations: 14 us -> 0.66 us
    dot_general x56 -> x0, matrix products: 146 us -> none  [the longest x8 29.2 us: update(): jnp.einsum('rkgd,ckd->kgrc', q_heads, k_group, preferred_element_type=jnp...]
    reduce_scatter x2 -> x0, waiting for transfers between devices: 120 us -> none  [the longest x1 64.4 us: on_device(): lax.psum_scatter(full_value, 'ctx', scatter_dimension=0, tiled=True)]
    pallas_call x0 -> x3, Pallas kernels: none -> 97.1 us  [the longest x1 47.4 us: exchange(): pl.pallas_call(exchange_kernel, name='exchange', out_shape=(jax.ShapeDtyp...]
    another operation x3 -> x0, loops' own time: 47.7 us -> none  [the longest x2 31.7 us: scan_keys(): return lax.scan(scan_step, state, shaped + (starts,))[0]]
    all_to_all x8 -> x0, waiting for transfers between devices: 46.3 us -> none  [the longest x1 10.1 us: on_device(): lax.all_to_all(by_target(regrouped[0]), 'ctx', split_axis=0, concat_axis=...]
    all_to_all x8 -> x0, starting transfers between devices: 40.3 us -> none  [the longest x1 8.48 us: on_device(): lax.all_to_all(key_rows, 'head', split_axis=1, concat_axis=0, tiled=True)]
    gather x5 -> x0, local copies, waits for them, and re-layouts: 28 us -> none  [the longest x1 25.7 us: slot_positions(): chosen = jnp.take(block_of.reshape(-1), source * shard_count + target)]
    reduce_sum x12 -> x0, other arithmetic: 26.5 us -> none  [the longest x8 25.5 us: update(): total = total * jnp.exp(peak - new_peak) + jnp.sum(weights, axis=3)]
  transfers between devices with their start and end apart: 12 -> 0, of which waited for: 9 -> 0; matrix products, arithmetic and copies ran while one was open for 20% -> 0% of each run, Pallas kernels for 0% -> 0%
where the time goes in v1:
time: 109 us; the launch traced here: 108 us
  Pallas kernels  97.1 us (89%)
  local copies, waits for them, and re-layouts  10.3 us (9%)
    pallas_call x1, Pallas kernels, exchange(): pl.pallas_call(exchange_kernel, name='exchange', out_shape=(jax.ShapeDtyp...  47.4 us
    pallas_call x1, Pallas kernels, attention(): pl.pallas_call(attention_kernel, name='attention', out_shape=(jax.ShapeDt...  27.6 us
    pallas_call x1, Pallas kernels, reduce(): pl.pallas_call(reduce_kernel, name='reduce', out_shape=(jax.ShapeDtypeStr...  22.1 us
    unnamed x16, local copies, waits for them, and re-layouts  10.3 us

profile of v1, /device:TPU:1, one launch (start us, length us, event | category | flops | bytes accessed | tf_op | source)
XLA Modules:
  0.0 108.1 jit_solution(17283049244023083927)
XLA Ops:
  0.6 47.4 %exchange.1 = (bf16[16,16,1024]{2,1,0:T(8,128)(2,1)}, bf16[16,16,1024]{2,1,0:T(8,128)(2,1)}, bf16[4096,128]{1,0:T(8,128)(2,1)}, bf16[4096,128]{1,0:T(8,128)(2,1)}) custom-call(s32[16,16]{1,0:T(8,128)} %route.3, bf16[2,16,8192]{2,1,0:T(8,128)(2,1)} %bitcast.6, bf16[32,1024]{1,0:T(8,128)(2,1)} %k.1, bf16[32,1024]{1,0:T(8,128)(2,1)} %v.1, ...), custom_call_target="tpu_custom_call" | custom-call | tf_op jit(solution)/shard_map/exchange/pallas_call | solution.py:211
  48.1 0.0 copy-start.1
  48.1 1.2 %copy-done.1 = bf16[4096,128]{1,0:T(8,128)(2,1)S(1)} copy-done((bf16[4096,128]{1,0:T(8,128)(2,1)S(1)}, bf16[4096,128]{1,0:T(8,128)(2,1)}, u32[]{:S(2)}) %copy-start.1) | copy-done | bytes 1048600
  49.3 0.0 copy-start.2
  49.3 1.2 %copy-done.2 = bf16[4096,128]{1,0:T(8,128)(2,1)S(1)} copy-done((bf16[4096,128]{1,0:T(8,128)(2,1)S(1)}, bf16[4096,128]{1,0:T(8,128)(2,1)}, u32[]{:S(2)}) %copy-start.2) | copy-done | bytes 1048600
  50.5 0.0 copy-start.3
  50.5 1.0 copy-done.3
  51.6 0.0 copy-start.4
  51.6 1.0 copy-done.4
  52.6 0.0 copy-start.5
  52.6 0.7 copy-done.5
  53.3 0.0 copy-start.6
  53.3 0.7 copy-done.6
  54.0 27.6 %attention.1 = (bf16[16,16,1024]{2,1,0:T(8,128)(2,1)}, f32[16,16,1024]{2,1,0:T(8,128)}, bf16[16,2,16,16,128]{4,3,2,1,0:T(8,128)(2,1)S(1)}) custom-call(s32[16,16]{1,0:T(8,128)S(1)} %copy-done.5, s32[8]{0:T(128)S(1)} %copy-done.6, bf16[16,16,1024]{2,1,0:T(8,128)(2,1)S(1)} %copy-done.3, bf16[16,16,1024]{2,1,0:T(8,128)(2,1)S(1)} %copy-done.4, ...), custom_call_target="tpu_custom_call" | custom-call | tf_op jit(solution)/shard_map/attention/pallas_call | solution.py:360
  81.5 0.0 copy-start
  81.5 1.3 %copy-done = bf16[16,2,16,16,128]{4,3,2,1,0:T(8,128)(2,1)} copy-done((bf16[16,2,16,16,128]{4,3,2,1,0:T(8,128)(2,1)}, bf16[16,2,16,16,128]{4,3,2,1,0:T(8,128)(2,1)S(1)}, u32[]{:S(2)}) %copy-start) | copy-done | bytes 2097176
  82.9 22.1 %reduce.1 = (f32[16,16,128]{2,1,0:T(8,128)}, f32[16,16,128]{2,1,0:T(8,128)}) custom-call(bf16[16,2,16,16,128]{4,3,2,1,0:T(8,128)(2,1)} %copy-done), custom_call_target="tpu_custom_call" | custom-call | tf_op jit(solution)/shard_map/reduce/pallas_call | solution.py:434
  104.9 1.6 %copy.12 = f32[256,128]{1,0:T(8,128)} copy(f32[256,128]{1,0:T(8,128)} %bitcast.9) | data formatting | bytes 262144
  106.5 1.6 %copy.13 = f32[256,128]{1,0:T(8,128)} copy(f32[256,128]{1,0:T(8,128)} %bitcast.8) | data formatting | bytes 262144
Async XLA Ops:
  48.1 1.2 %copy-start.1 = (bf16[4096,128]{1,0:T(8,128)(2,1)S(1)}, bf16[4096,128]{1,0:T(8,128)(2,1)}, u32[]{:S(2)}) copy-start(bf16[4096,128]{1,0:T(8,128)(2,1)} %get-tuple-element.15.k) | copy-start | bytes 3145732
  49.3 1.2 %copy-start.2 = (bf16[4096,128]{1,0:T(8,128)(2,1)S(1)}, bf16[4096,128]{1,0:T(8,128)(2,1)}, u32[]{:S(2)}) copy-start(bf16[4096,128]{1,0:T(8,128)(2,1)} %get-tuple-element.16.v) | copy-start | bytes 3145732
  50.5 1.0 copy-start.3
  51.6 1.0 copy-start.4
  52.6 0.7 copy-start.5
  53.3 0.7 copy-start.6
  81.5 1.3 %copy-start = (bf16[16,2,16,16,128]{4,3,2,1,0:T(8,128)(2,1)}, bf16[16,2,16,16,128]{4,3,2,1,0:T(8,128)(2,1)S(1)}, u32[]{:S(2)}) copy-start(bf16[16,2,16,16,128]{4,3,2,1,0:T(8,128)(2,1)S(1)} %get-tuple-element.19.part) | copy-start | bytes 6291460

commit v2 on v1

--- a/solution.py
+++ b/solution.py
@@ -1,3 +1,4 @@
+import functools
 import math
 
 import jax
@@ -18,7 +19,8 @@
 COLS = GROUP * HD
 
 SPAN = 4
-LANES = SPAN * GROUP * BLOCK
+WIDTH = GROUP * BLOCK
+LANES = SPAN * WIDTH
 NEGATIVE = -1e30
 FLOOR = -0.5e30
 SCALE = 1.0 / math.sqrt(HD)
@@ -97,7 +99,8 @@
         pltpu.make_async_copy(k.at[:, own_cols], ko.at[kv_rows], local.at[0]),
         pltpu.make_async_copy(v.at[:, own_cols], vo.at[kv_rows], local.at[1]),
     ]
-    for a, (src, dst) in enumerate(((q, xq), (g, xg))):
+
+    def first(a, src, dst):
         for jz, jy in head_peers:
             j = jz * 2 + jy
             peer = head_of(z + jz, yh + jy)
@@ -108,8 +111,11 @@
         cols = pl.ds(pl.multiple_of(h * COLS, COLS), COLS)
         own.append(pltpu.make_async_copy(
             src.at[:, :, cols], dst.at[pl.ds(h * 2, 2)], local.at[2 + a]))
+        own[-1].start()
+
     for copy in own:
         copy.start()
+    first(0, q, xq)
 
     kv = (ko, vo)
 
@@ -140,6 +146,8 @@
         go_remote(ring(a, 0, 0, 0, 1))
         go_remote(ring(a, 0, 0, 1, 0))
         go_remote(ring(a, 0, 0, -1, 0))
+    first(1, g, xg)
+    for a in range(2):
         go_remote(partner(a, 0, 0))
 
     def second(a, stage, send, out):
@@ -165,27 +173,32 @@
                 send.at[d], out.at[c], p2s.at[a, j], p2r.at[a, j], d, h)))
         return mine, copies
 
+    def sides(dy):
+        arrived(0, 3, dy)
+        go_remote(ring(0, 3, dy, 1, 0))
+        arrived(1, 1, dy)
+        go_remote(ring(1, 1, dy, -1, 0))
+        arrived(0, 1, dy)
+        arrived(1, 3, dy)
+        for a in range(2):
+            go_remote(partner(a, 3, dy))
+            go_remote(partner(a, 1, dy))
+
+    sides(0)
     for a in range(2):
         arrived(a, 0, 1)
         go_remote(ring(a, 0, 1, 1, 0))
         go_remote(ring(a, 0, 1, -1, 0))
         go_remote(partner(a, 0, 1))
     mine_q, p2q = second(0, xq, sq, qo)
-    for dy in range(2):
-        for a in range(2):
-            arrived(a, 3, dy)
-            if a == 0:
-                go_remote(ring(a, 3, dy, 1, 0))
-            go_remote(partner(a, 3, dy))
-            arrived(a, 1, dy)
-            if a == 1:
-                go_remote(ring(a, 1, dy, -1, 0))
-            go_remote(partner(a, 1, dy))
+    sides(1)
+    for a in range(2):
+        arrived(a, 2, 0)
+        go_remote(partner(a, 2, 0))
     mine_g, p2g = second(1, xg, sg, go)
-    for dy in range(2):
-        for a in range(2):
-            arrived(a, 2, dy)
-            go_remote(partner(a, 2, dy))
+    for a in range(2):
+        arrived(a, 2, 1)
+        go_remote(partner(a, 2, 1))
     mine_q.wait()
     mine_g.wait()
 
@@ -239,9 +252,18 @@
 
 
 def attention_kernel(
-    route, docs, q, g, k, v, att, dq, dkv,
-    s_buf, kt, vt, dk_acc, dv_acc, ot_acc, dqt_acc, starts,
+    route, docs, q_hbm, g_hbm, k_hbm, v_hbm, att_hbm, dq_hbm, dkv_hbm,
+    q, g, k, v, att, dq, dkv,
+    s_buf, kt, vt, dk_acc, dv_acc, ot_acc, dqt_acc, starts, load, store,
 ):
+    loads = [
+        pltpu.make_async_copy(k_hbm, k, load.at[0]),
+        pltpu.make_async_copy(v_hbm, v, load.at[1]),
+        pltpu.make_async_copy(q_hbm, q, load.at[2]),
+        pltpu.make_async_copy(g_hbm, g, load.at[3]),
+    ]
+    for copy in loads:
+        copy.start()
     c = lax.axis_index("ctx")
     ends = []
     total = jnp.int32(0)
@@ -257,16 +279,17 @@
         return carry
 
     lax.fori_loop(0, SHARDS, find, 0)
+    loads[0].wait()
+    loads[1].wait()
 
     def prepare(t, carry):
-        kt[t] = k[pl.ds(t * ROWS, ROWS), :].T
-        vt[t] = v[pl.ds(t * ROWS, ROWS), :].T
-        zero = jnp.zeros((ROWS, HD), F32)
-        dk_acc[pl.ds(t * ROWS, ROWS), :] = zero
-        dv_acc[pl.ds(t * ROWS, ROWS), :] = zero
+        kt[t] = k[t].T
+        vt[t] = v[t].T
         return carry
 
     lax.fori_loop(0, SHARDS, prepare, 0)
+    loads[2].wait()
+    loads[3].wait()
 
     def stack(ref, first):
         parts = []
@@ -275,8 +298,15 @@
             parts += [rows[:, n * HD:(n + 1) * HD] for n in range(GROUP)]
         return jnp.concatenate(parts, axis=0)
 
-    lane = lax.broadcasted_iota(jnp.int32, (1, GROUP * BLOCK), 1)
-    within = lax.rem(lane, BLOCK)
+    def outgoing(n):
+        rows = pl.ds(n * SPAN, SPAN)
+        return (
+            pltpu.make_async_copy(att.at[rows], att_hbm.at[rows], store.at[0]),
+            pltpu.make_async_copy(dq.at[rows], dq_hbm.at[rows], store.at[1]),
+        )
+
+    within = lax.rem(lax.broadcasted_iota(jnp.int32, (1, WIDTH), 1), BLOCK)
+    key = lax.broadcasted_iota(jnp.int32, (ROWS, WIDTH), 0)
 
     def group(n, carry):
         first = n * SPAN
@@ -287,35 +317,75 @@
         q_pos = jnp.concatenate([within + starts[first + i] for i in range(SPAN)], axis=1)
         q_doc = jnp.zeros_like(q_pos)
         low = jnp.int32(0)
+        high = jnp.int32(0)
         p_first = starts[first]
+        p_last = starts[first + SPAN - 1] + BLOCK - 1
         for end in ends:
             q_doc = jnp.where(q_pos >= end, end, q_doc)
             low = jnp.where(p_first >= end, end, low)
+            high = jnp.where(p_last >= end, end, high)
         t_low = low // ROWS
-        t_high = first + SPAN
-        key = lax.broadcasted_iota(jnp.int32, (ROWS, LANES), 0)
+        t_full = jnp.minimum((high + ROWS - 1) // ROWS, first)
+        reach = (q_pos - q_doc).astype(jnp.uint32)
+
+        def scores(t, lane):
+            s = jnp.dot(k[t], qt[:, lane:], preferred_element_type=F32)
+            return s * (SCALE * LOG2E)
+
+        def masked(t, lane):
+            s = scores(t, lane)
+            offset = t * ROWS - q_doc[:, lane:]
+            parts = []
+            for i in range(0, LANES - lane, WIDTH):
+                past = (key + offset[:, i:i + WIDTH]).astype(jnp.uint32)
+                seen = past <= reach[:, lane + i:lane + i + WIDTH]
+                parts.append(jnp.where(seen, s[:, i:i + WIDTH], NEGATIVE))
+            return jnp.concatenate(parts, axis=1)
+
         ot_acc[...] = jnp.zeros_like(ot_acc)
         dqt_acc[...] = jnp.zeros_like(dqt_acc)
 
-        def forward(t, carried):
-            peak, mass = carried
-            s = jnp.dot(k[pl.ds(t * ROWS, ROWS), :], qt, preferred_element_type=F32)
-            base = t * ROWS
-            seen = (key >= q_doc - base) & (key <= q_pos - base)
-            s = jnp.where(seen, s * (SCALE * LOG2E), NEGATIVE)
-            s_buf[t] = s
-            new_peak = jnp.maximum(peak, jnp.max(s, axis=0, keepdims=True))
-            p = jnp.exp2(s - new_peak)
-            fade = jnp.exp2(peak - new_peak)
-            mass = mass * fade + jnp.sum(p, axis=0, keepdims=True)
-            ot_acc[...] = ot_acc[...] * fade + jnp.dot(
-                vt[t], p.astype(BF), preferred_element_type=F32)
-            return new_peak, mass
+        def forward(produce):
+            def step(t, carried):
+                peak, mass = carried
+                s = produce(t, 0)
+                s_buf[t] = s
+                new_peak = jnp.maximum(peak, jnp.max(s, axis=0, keepdims=True))
+                p = jnp.exp2(s - new_peak)
+                fade = jnp.exp2(peak - new_peak)
+                mass = mass * fade + jnp.sum(p, axis=0, keepdims=True)
+                ot_acc[...] = ot_acc[...] * fade + jnp.dot(
+                    vt[t], p.astype(BF), preferred_element_type=F32)
+                return new_peak, mass
+
+            return step
 
         peak, mass = lax.fori_loop(
-            t_low, t_high, forward,
+            t_low, t_full, forward(masked),
             (jnp.full((1, LANES), FLOOR, F32), jnp.zeros((1, LANES), F32)))
-        lse = peak + jnp.log2(mass)
+        peak, mass = lax.fori_loop(t_full, first, forward(scores), (peak, mass))
+
+        tops = [[peak[:, i * WIDTH:(i + 1) * WIDTH]] for i in range(SPAN)]
+        for e in range(SPAN):
+            s = masked(first + e, e * WIDTH)
+            s_buf[first + e, :, e * WIDTH:] = s
+            top = jnp.max(s, axis=0, keepdims=True)
+            for i in range(e, SPAN):
+                tops[i].append(top[:, (i - e) * WIDTH:(i - e + 1) * WIDTH])
+        new_peak = jnp.concatenate([functools.reduce(jnp.maximum, t) for t in tops], axis=1)
+        fade = jnp.exp2(peak - new_peak)
+        mass = mass * fade
+        masses = [[mass[:, i * WIDTH:(i + 1) * WIDTH]] for i in range(SPAN)]
+        ot_acc[...] = ot_acc[...] * fade
+        for e in range(SPAN):
+            p = jnp.exp2(s_buf[first + e, :, e * WIDTH:] - new_peak[:, e * WIDTH:])
+            add = jnp.sum(p, axis=0, keepdims=True)
+            for i in range(e, SPAN):
+                masses[i].append(add[:, (i - e) * WIDTH:(i - e + 1) * WIDTH])
+            ot_acc[:, e * WIDTH:] += jnp.dot(
+                vt[first + e], p.astype(BF), preferred_element_type=F32)
+        mass = jnp.concatenate([functools.reduce(jnp.add, t) for t in masses], axis=1)
+        lse = new_peak + jnp.log2(mass)
         ot = (ot_acc[...] * (1.0 / mass)).astype(BF)
         delta = jnp.sum(gt.astype(F32) * ot.astype(F32), axis=0, keepdims=True)
         o = ot.T
@@ -324,22 +394,34 @@
                 r = (i * GROUP + m) * BLOCK
                 att[first + i, :, m * HD:(m + 1) * HD] = o[r:r + BLOCK]
 
+        def pull(t, lane):
+            p = jnp.exp2(s_buf[t, :, lane:] - lse[:, lane:])
+            dp = jnp.dot(v[t], gt[:, lane:], preferred_element_type=F32)
+            ds = (p * (dp - delta[:, lane:])).astype(BF)
+            grad_v = jnp.dot(p.astype(BF), gg[lane:], preferred_element_type=F32)
+            grad_k = jnp.dot(ds, qg[lane:], preferred_element_type=F32)
+            dqt_acc[:, lane:] += jnp.dot(kt[t], ds, preferred_element_type=F32)
+            return grad_v, grad_k
+
+        for e in range(SPAN):
+            grad_v, grad_k = pull(first + e, e * WIDTH)
+            dv_acc[first + e] = grad_v
+            dk_acc[first + e] = grad_k
+
         def backward(t, carried):
-            rows = pl.ds(t * ROWS, ROWS)
-            p = jnp.exp2(s_buf[t] - lse)
-            dp = jnp.dot(v[rows, :], gt, preferred_element_type=F32)
-            ds = (p * (dp - delta)).astype(BF)
-            dv_acc[rows, :] += jnp.dot(p.astype(BF), gg, preferred_element_type=F32)
-            dk_acc[rows, :] += jnp.dot(ds, qg, preferred_element_type=F32)
-            dqt_acc[...] += jnp.dot(kt[t], ds, preferred_element_type=F32)
+            grad_v, grad_k = pull(t, 0)
+            dv_acc[t] += grad_v
+            dk_acc[t] += grad_k
             return carried
 
-        lax.fori_loop(t_low, t_high, backward, 0)
+        lax.fori_loop(t_low, first, backward, 0)
         grad = dqt_acc[...].T * SCALE
         for i in range(SPAN):
             for m in range(GROUP):
                 r = (i * GROUP + m) * BLOCK
                 dq[first + i, :, m * HD:(m + 1) * HD] = grad[r:r + BLOCK]
+        for copy in outgoing(n):
+            copy.start()
         return carry
 
     lax.fori_loop(0, SHARDS // SPAN, group, 0)
@@ -347,13 +429,17 @@
     def regroup(s, carry):
         for b in range(SHARDS):
             d = route[s, b]
-            to = lax.rem(d, 2) * 8 + d // 2
-            rows = pl.ds(s * ROWS + b * BLOCK, BLOCK)
-            dkv[to, 0, s] = (dk_acc[rows, :] * SCALE).astype(BF)
-            dkv[to, 1, s] = dv_acc[rows, :].astype(BF)
+            rows = slice(b * BLOCK, (b + 1) * BLOCK)
+            dkv[d, 0, s] = (dk_acc[s, rows] * SCALE).astype(BF)
+            dkv[d, 1, s] = dv_acc[s, rows].astype(BF)
         return carry
 
     lax.fori_loop(0, SHARDS, regroup, 0)
+    last = pltpu.make_async_copy(dkv, dkv_hbm, load.at[0])
+    last.start()
+    pltpu.make_async_copy(att, att_hbm, store.at[0]).wait()
+    pltpu.make_async_copy(dq, dq_hbm, store.at[1]).wait()
+    last.wait()
 
 
 def attention(route, docs, q, g, k, v):
@@ -365,23 +451,31 @@
             jax.ShapeDtypeStruct((SHARDS, BLOCK, COLS), F32),
             jax.ShapeDtypeStruct((SHARDS, 2, SHARDS, BLOCK, HD), BF),
         ),
-        in_specs=[SMEM, SMEM, VMEM, VMEM, VMEM, VMEM],
-        out_specs=(VMEM, VMEM, VMEM),
+        in_specs=[SMEM, SMEM, ANY, ANY, ANY, ANY],
+        out_specs=(ANY, ANY, ANY),
         scratch_shapes=[
+            pltpu.VMEM((SHARDS, BLOCK, COLS), BF),
+            pltpu.VMEM((SHARDS, BLOCK, COLS), BF),
+            pltpu.VMEM((SHARDS, ROWS, HD), BF),
+            pltpu.VMEM((SHARDS, ROWS, HD), BF),
+            pltpu.VMEM((SHARDS, BLOCK, COLS), BF),
+            pltpu.VMEM((SHARDS, BLOCK, COLS), F32),
+            pltpu.VMEM((SHARDS, 2, SHARDS, BLOCK, HD), BF),
             pltpu.VMEM((SHARDS, ROWS, LANES), F32),
             pltpu.VMEM((SHARDS, HD, ROWS), BF),
             pltpu.VMEM((SHARDS, HD, ROWS), BF),
-            pltpu.VMEM((SEQ, HD), F32),
-            pltpu.VMEM((SEQ, HD), F32),
+            pltpu.VMEM((SHARDS, ROWS, HD), F32),
+            pltpu.VMEM((SHARDS, ROWS, HD), F32),
             pltpu.VMEM((HD, LANES), F32),
             pltpu.VMEM((HD, LANES), F32),
             pltpu.SMEM((SHARDS,), jnp.int32),
+            pltpu.SemaphoreType.DMA((4,)),
+            pltpu.SemaphoreType.DMA((2,)),
         ],
-        compiler_params=pltpu.CompilerParams(vmem_limit_bytes=48 << 20),
     )(route, docs, q, g, k, v)
 
 
-def reduce_kernel(part, dk, dv, mate, chip, total, s1, r1, s2, r2):
+def reduce_kernel(part, chip, keep, mine, mate, kept, s1, r1, s2, r2, local):
     c = lax.axis_index("ctx")
     h = lax.axis_index("head")
     x, yl, core = c // 4, lax.rem(c // 2, 2), lax.rem(c, 2)
@@ -389,6 +483,16 @@
     order = peers + [(0, 0)]
     other = ctx_of(x, yl, core + 1)
 
+    def place(jx, jy):
+        return lax.rem(x + jx, 4) * 2 + lax.rem(yl + jy, 2)
+
+    loads = []
+    for jx, jy in order:
+        t = place(jx, jy)
+        copy = pltpu.make_async_copy(part.at[t * 2 + core], mine.at[t], local.at[jx * 2 + jy])
+        copy.start()
+        loads.append(copy)
+
     barrier = pltpu.get_barrier_semaphore()
     pl.semaphore_signal(barrier, inc=1, device_id=(other, h), device_id_type=MESH)
     for jx, jy in peers:
@@ -396,37 +500,35 @@
             barrier, inc=1, device_id=(ctx_of(x + jx, yl + jy, core), h), device_id_type=MESH)
     pl.semaphore_wait(barrier, len(peers) + 1)
 
-    def place(jx, jy):
-        return lax.rem(x + jx, 4) * 2 + lax.rem(yl + jy, 2)
-
     first = []
     for jx, jy in order:
         j = jx * 2 + jy
         t = place(jx, jy)
-        copy = remote(part.at[(1 - core) * 8 + t], mate.at[t], s1.at[j], r1.at[j], other, h)
+        copy = remote(part.at[t * 2 + 1 - core], mate.at[t], s1.at[j], r1.at[j], other, h)
         copy.start()
         first.append(copy)
     second = []
-    for (jx, jy), copy in zip(order, first):
+    for (jx, jy), copy, load in zip(order, first, loads):
         j = jx * 2 + jy
         t = place(jx, jy)
+        load.wait()
         copy.wait_recv()
-        pair = part[core * 8 + t].astype(F32) + mate[t].astype(F32)
+        pair = mine[t].astype(F32) + mate[t].astype(F32)
         if (jx, jy) == (0, 0):
-            total[...] = pair
+            kept[...] = pair
         else:
             mate[t] = pair.astype(BF)
-            copy = remote(mate.at[t], chip.at[j], s2.at[j], r2.at[j],
+            copy = remote(mate.at[t], chip.at[j - 1], s2.at[j], r2.at[j],
                           ctx_of(x + jx, yl + jy, core), h)
             copy.start()
             second.append(copy)
-    for copy, (jx, jy) in zip(second, peers):
+    out = pltpu.make_async_copy(kept, keep, local.at[0])
+    out.start()
+    for copy in second:
         copy.wait_recv()
-        total[...] += chip[jx * 2 + jy].astype(F32)
-    dk[...] = total[0]
-    dv[...] = total[1]
     for copy in first + second:
         copy.wait_send()
+    out.wait()
 
 
 def reduce(part):
@@ -435,11 +537,11 @@
         reduce_kernel,
         name="reduce",
         out_shape=(
-            jax.ShapeDtypeStruct((SHARDS, BLOCK, HD), F32),
-            jax.ShapeDtypeStruct((SHARDS, BLOCK, HD), F32),
+            jax.ShapeDtypeStruct((7,) + shape, BF),
+            jax.ShapeDtypeStruct(shape, F32),
         ),
-        in_specs=[VMEM],
-        out_specs=(VMEM, VMEM),
+        in_specs=[ANY],
+        out_specs=(ANY, ANY),
         scratch_shapes=[
             pltpu.VMEM((8,) + shape, BF),
             pltpu.VMEM((8,) + shape, BF),
@@ -448,9 +550,33 @@
             pltpu.SemaphoreType.DMA((8,)),
             pltpu.SemaphoreType.DMA((8,)),
             pltpu.SemaphoreType.DMA((8,)),
+            pltpu.SemaphoreType.DMA((8,)),
         ],
         compiler_params=pltpu.CompilerParams(collective_id=1, has_side_effects=True),
     )(part)
+
+
+def finish_kernel(chip, keep, dk, dv):
+    for a, out in enumerate((dk, dv)):
+        def add(s, carry):
+            total = keep[a, s]
+            for j in range(7):
+                total = total + chip[j, a, s].astype(F32)
+            out[s] = total
+            return carry
+
+        lax.fori_loop(0, SHARDS, add, 0)
+
+
+def finish(chip, keep):
+    out = jax.ShapeDtypeStruct((SHARDS, BLOCK, HD), F32)
+    return pl.pallas_call(
+        finish_kernel,
+        name="finish",
+        out_shape=(out, out),
+        in_specs=[VMEM, VMEM],
+        out_specs=(VMEM, VMEM),
+    )(chip, keep)
 
 
 def on_device(queries, key_rows, value_rows, cotangent, doc_lengths, block_route):
@@ -461,8 +587,9 @@
         value_rows,
         cotangent.reshape(2, BLOCK, HEADS * COLS),
     )
-    att, dq, part = attention(block_route, doc_lengths, q, g, k, v)
-    dk, dv = reduce(part)
+    att, dq, part = attention(
+        block_route, doc_lengths, q, g, k.reshape(SHARDS, ROWS, HD), v.reshape(SHARDS, ROWS, HD))
+    dk, dv = finish(*reduce(part))
     return (
         att.reshape(ROWS, COLS),
         dq.reshape(ROWS, COLS),

time: 109 us -> 90.8 us (0.83)
  local copies, waits for them, and re-layouts: 10.3 us -> 0 us
  Pallas kernels: 97.1 us -> 89.9 us
    unnamed x16 -> x0, local copies, waits for them, and re-layouts: 10.3 us -> none
    pallas_call x1, Pallas kernels: 47.4 us -> 40.8 us  [exchange(): pl.pallas_call(exchange_kernel, name='exchange', out_shape=(jax.ShapeDtyp...]
    pallas_call x0 -> x1, Pallas kernels: none -> 2.25 us  [finish(): pl.pallas_call(finish_kernel, name='finish', out_shape=(out, out), in_spe...]
    pallas_call x1, Pallas kernels: 22.1 us -> 20.3 us  [reduce(): pl.pallas_call(reduce_kernel, name='reduce', out_shape=(jax.ShapeDtypeStr...]
where the time goes in v2:
time: 90.8 us; the launch traced here: 90.6 us
  Pallas kernels  89.9 us (99%)
    pallas_call x1, Pallas kernels, exchange(): pl.pallas_call(exchange_kernel, name='exchange', out_shape=(jax.ShapeDtyp...  40.8 us
    pallas_call x1, Pallas kernels, attention(): pl.pallas_call(attention_kernel, name='attention', out_shape=(jax.ShapeDt...  26.6 us
    pallas_call x1, Pallas kernels, reduce(): pl.pallas_call(reduce_kernel, name='reduce', out_shape=(jax.ShapeDtypeStr...  20.3 us
    pallas_call x1, Pallas kernels, finish(): pl.pallas_call(finish_kernel, name='finish', out_shape=(out, out), in_spe...  2.25 us

profile of v2, /device:TPU:1, one launch (start us, length us, event | category | flops | bytes accessed | tf_op | source)
XLA Modules:
  0.0 90.6 jit_solution(10222808227701691322)
XLA Ops:
  0.6 40.8 %exchange.1 = (bf16[16,16,1024]{2,1,0:T(8,128)(2,1)}, bf16[16,16,1024]{2,1,0:T(8,128)(2,1)}, bf16[4096,128]{1,0:T(8,128)(2,1)}, bf16[4096,128]{1,0:T(8,128)(2,1)}) custom-call(s32[16,16]{1,0:T(8,128)} %route.3, bf16[2,16,8192]{2,1,0:T(8,128)(2,1)} %bitcast.10, bf16[32,1024]{1,0:T(8,128)(2,1)} %k.1, bf16[32,1024]{1,0:T(8,128)(2,1)} %v.1, ...), custom_call_target="tpu_custom_call" | custom-call | tf_op jit(solution)/shard_map/exchange/pallas_call | solution.py:224
  41.4 26.6 %attention.1 = (bf16[16,16,1024]{2,1,0:T(8,128)(2,1)}, f32[16,16,1024]{2,1,0:T(8,128)}, bf16[16,2,16,16,128]{4,3,2,1,0:T(8,128)(2,1)}) custom-call(s32[16,16]{1,0:T(8,128)} %route.3, s32[8]{0:T(128)} %docs.1, bf16[16,16,1024]{2,1,0:T(8,128)(2,1)} %get-tuple-element.15.q_hbm, bf16[16,16,1024]{2,1,0:T(8,128)(2,1)} %get-tuple-element.16.g_hbm, ...), custom_call_target="tpu_custom_call" | custom-call | tf_op jit(solution)/shard_map/attention/pallas_call | solution.py:446
  68.1 20.3 %reduce.1 = (bf16[7,2,16,16,128]{4,3,2,1,0:T(8,128)(2,1)}, f32[2,16,16,128]{3,2,1,0:T(8,128)}) custom-call(bf16[16,2,16,16,128]{4,3,2,1,0:T(8,128)(2,1)} %get-tuple-element.21.part), custom_call_target="tpu_custom_call" | custom-call | tf_op jit(solution)/shard_map/reduce/pallas_call | solution.py:536
  88.3 2.2 %finish.1 = (f32[16,16,128]{2,1,0:T(8,128)}, f32[16,16,128]{2,1,0:T(8,128)}) custom-call(bf16[7,2,16,16,128]{4,3,2,1,0:T(8,128)(2,1)} %get-tuple-element.22.chip, f32[2,16,16,128]{3,2,1,0:T(8,128)} %get-tuple-element.23.keep), custom_call_target="tpu_custom_call" | custom-call | tf_op jit(solution)/shard_map/finish/pallas_call | solution.py:573

commit v3 on v2

--- a/solution.py
+++ b/solution.py
@@ -316,27 +316,25 @@
         gt = gg.T
         q_pos = jnp.concatenate([within + starts[first + i] for i in range(SPAN)], axis=1)
         q_doc = jnp.zeros_like(q_pos)
-        low = jnp.int32(0)
-        high = jnp.int32(0)
-        p_first = starts[first]
-        p_last = starts[first + SPAN - 1] + BLOCK - 1
+        marks = [starts[first], starts[first + 1], starts[first + 2],
+                 starts[first + SPAN - 1] + BLOCK - 1]
+        lows = [jnp.int32(0)] * 4
         for end in ends:
             q_doc = jnp.where(q_pos >= end, end, q_doc)
-            low = jnp.where(p_first >= end, end, low)
-            high = jnp.where(p_last >= end, end, high)
-        t_low = low // ROWS
-        t_full = jnp.minimum((high + ROWS - 1) // ROWS, first)
+            lows = [jnp.where(mark >= end, end, low) for mark, low in zip(marks, lows)]
+        t_one, t_two, t_low = [jnp.minimum(low // ROWS, first) for low in lows[:3]]
+        t_full = jnp.minimum((lows[3] + ROWS - 1) // ROWS, first)
         reach = (q_pos - q_doc).astype(jnp.uint32)
 
-        def scores(t, lane):
-            s = jnp.dot(k[t], qt[:, lane:], preferred_element_type=F32)
+        def scores(t, lane, stop=LANES):
+            s = jnp.dot(k[t], qt[:, lane:stop], preferred_element_type=F32)
             return s * (SCALE * LOG2E)
 
-        def masked(t, lane):
-            s = scores(t, lane)
-            offset = t * ROWS - q_doc[:, lane:]
+        def masked(t, lane, stop=LANES):
+            s = scores(t, lane, stop)
+            offset = t * ROWS - q_doc[:, lane:stop]
             parts = []
-            for i in range(0, LANES - lane, WIDTH):
+            for i in range(0, stop - lane, WIDTH):
                 past = (key + offset[:, i:i + WIDTH]).astype(jnp.uint32)
                 seen = past <= reach[:, lane + i:lane + i + WIDTH]
                 parts.append(jnp.where(seen, s[:, i:i + WIDTH], NEGATIVE))
@@ -345,25 +343,29 @@
         ot_acc[...] = jnp.zeros_like(ot_acc)
         dqt_acc[...] = jnp.zeros_like(dqt_acc)
 
-        def forward(produce):
+        def forward(produce, stop=LANES):
             def step(t, carried):
                 peak, mass = carried
-                s = produce(t, 0)
-                s_buf[t] = s
-                new_peak = jnp.maximum(peak, jnp.max(s, axis=0, keepdims=True))
+                s = produce(t, 0, stop)
+                s_buf[t, :, :stop] = s
+                new_peak = jnp.maximum(peak[:, :stop], jnp.max(s, axis=0, keepdims=True))
                 p = jnp.exp2(s - new_peak)
-                fade = jnp.exp2(peak - new_peak)
-                mass = mass * fade + jnp.sum(p, axis=0, keepdims=True)
-                ot_acc[...] = ot_acc[...] * fade + jnp.dot(
+                fade = jnp.exp2(peak[:, :stop] - new_peak)
+                new_mass = mass[:, :stop] * fade + jnp.sum(p, axis=0, keepdims=True)
+                ot_acc[:, :stop] = ot_acc[:, :stop] * fade + jnp.dot(
                     vt[t], p.astype(BF), preferred_element_type=F32)
-                return new_peak, mass
+                if stop < LANES:
+                    new_peak = jnp.concatenate([new_peak, peak[:, stop:]], axis=1)
+                    new_mass = jnp.concatenate([new_mass, mass[:, stop:]], axis=1)
+                return new_peak, new_mass
 
             return step
 
-        peak, mass = lax.fori_loop(
-            t_low, t_full, forward(masked),
-            (jnp.full((1, LANES), FLOOR, F32), jnp.zeros((1, LANES), F32)))
-        peak, mass = lax.fori_loop(t_full, first, forward(scores), (peak, mass))
+        state = (jnp.full((1, LANES), FLOOR, F32), jnp.zeros((1, LANES), F32))
+        state = lax.fori_loop(t_one, t_two, forward(masked, WIDTH), state)
+        state = lax.fori_loop(t_two, t_low, forward(masked, 2 * WIDTH), state)
+        state = lax.fori_loop(t_low, t_full, forward(masked), state)
+        peak, mass = lax.fori_loop(t_full, first, forward(scores), state)
 
         tops = [[peak[:, i * WIDTH:(i + 1) * WIDTH]] for i in range(SPAN)]
         for e in range(SPAN):
@@ -394,13 +396,13 @@
                 r = (i * GROUP + m) * BLOCK
                 att[first + i, :, m * HD:(m + 1) * HD] = o[r:r + BLOCK]
 
-        def pull(t, lane):
-            p = jnp.exp2(s_buf[t, :, lane:] - lse[:, lane:])
-            dp = jnp.dot(v[t], gt[:, lane:], preferred_element_type=F32)
-            ds = (p * (dp - delta[:, lane:])).astype(BF)
-            grad_v = jnp.dot(p.astype(BF), gg[lane:], preferred_element_type=F32)
-            grad_k = jnp.dot(ds, qg[lane:], preferred_element_type=F32)
-            dqt_acc[:, lane:] += jnp.dot(kt[t], ds, preferred_element_type=F32)
+        def pull(t, lane, stop=LANES):
+            p = jnp.exp2(s_buf[t, :, lane:stop] - lse[:, lane:stop])
+            dp = jnp.dot(v[t], gt[:, lane:stop], preferred_element_type=F32)
+            ds = (p * (dp - delta[:, lane:stop])).astype(BF)
+            grad_v = jnp.dot(p.astype(BF), gg[lane:stop], preferred_element_type=F32)
+            grad_k = jnp.dot(ds, qg[lane:stop], preferred_element_type=F32)
+            dqt_acc[:, lane:stop] += jnp.dot(kt[t], ds, preferred_element_type=F32)
             return grad_v, grad_k
 
         for e in range(SPAN):
@@ -408,13 +410,18 @@
             dv_acc[first + e] = grad_v
             dk_acc[first + e] = grad_k
 
-        def backward(t, carried):
-            grad_v, grad_k = pull(t, 0)
-            dv_acc[t] += grad_v
-            dk_acc[t] += grad_k
-            return carried
-
-        lax.fori_loop(t_low, first, backward, 0)
+        def backward(stop):
+            def step(t, carried):
+                grad_v, grad_k = pull(t, 0, stop)
+                dv_acc[t] += grad_v
+                dk_acc[t] += grad_k
+                return carried
+
+            return step
+
+        lax.fori_loop(t_one, t_two, backward(WIDTH), 0)
+        lax.fori_loop(t_two, t_low, backward(2 * WIDTH), 0)
+        lax.fori_loop(t_low, first, backward(LANES), 0)
         grad = dqt_acc[...].T * SCALE
         for i in range(SPAN):
             for m in range(GROUP):
@@ -475,81 +482,122 @@
     )(route, docs, q, g, k, v)
 
 
-def reduce_kernel(part, chip, keep, mine, mate, kept, s1, r1, s2, r2, local):
+def reduce_kernel(
+    part, chip, keep, mine, mate, hold, kept, from_y, from_x,
+    s1, r1, sy, ry, sx, rx, s2, r2, local,
+):
     c = lax.axis_index("ctx")
     h = lax.axis_index("head")
     x, yl, core = c // 4, lax.rem(c // 2, 2), lax.rem(c, 2)
-    peers = [(jx, jy) for jx in range(4) for jy in range(2) if (jx, jy) != (0, 0)]
-    order = peers + [(0, 0)]
     other = ctx_of(x, yl, core + 1)
-
-    def place(jx, jy):
-        return lax.rem(x + jx, 4) * 2 + lax.rem(yl + jy, 2)
+    across = ctx_of(x, yl + 1, core)
+    far = (2, 1, 3, 0)
+    order = [(dx, dy) for dx in far for dy in (1, 0)]
+
+    def along(dx):
+        return ctx_of(x + dx, yl, core)
+
+    def place(dx, dy):
+        return lax.rem(x + dx, 4) * 2 + lax.rem(yl + dy, 2)
 
     loads = []
-    for jx, jy in order:
-        t = place(jx, jy)
-        copy = pltpu.make_async_copy(part.at[t * 2 + core], mine.at[t], local.at[jx * 2 + jy])
+    for i, (dx, dy) in enumerate(order):
+        t = place(dx, dy)
+        copy = pltpu.make_async_copy(part.at[t * 2 + core], mine.at[t], local.at[i])
         copy.start()
         loads.append(copy)
 
     barrier = pltpu.get_barrier_semaphore()
-    pl.semaphore_signal(barrier, inc=1, device_id=(other, h), device_id_type=MESH)
-    for jx, jy in peers:
-        pl.semaphore_signal(
-            barrier, inc=1, device_id=(ctx_of(x + jx, yl + jy, core), h), device_id_type=MESH)
-    pl.semaphore_wait(barrier, len(peers) + 1)
-
-    first = []
-    for jx, jy in order:
-        j = jx * 2 + jy
-        t = place(jx, jy)
-        copy = remote(part.at[t * 2 + 1 - core], mate.at[t], s1.at[j], r1.at[j], other, h)
+    for peer in (other, across, along(1), along(2), along(3)):
+        pl.semaphore_signal(barrier, inc=1, device_id=(peer, h), device_id_type=MESH)
+    pl.semaphore_wait(barrier, 5)
+
+    sent = []
+
+    def start(*args):
+        copy = remote(*args, h)
         copy.start()
-        first.append(copy)
-    second = []
-    for (jx, jy), copy, load in zip(order, first, loads):
-        j = jx * 2 + jy
-        t = place(jx, jy)
+        sent.append(copy)
+        return copy
+
+    pairs = []
+    for i, (dx, dy) in enumerate(order):
+        t = place(dx, dy)
+        pairs.append(start(part.at[t * 2 + 1 - core], mate.at[t], s1.at[i], r1.at[i], other))
+
+    for (dx, dy), pair, load in zip(order, pairs, loads):
+        t = place(dx, dy)
         load.wait()
-        copy.wait_recv()
-        pair = mine[t].astype(F32) + mate[t].astype(F32)
-        if (jx, jy) == (0, 0):
-            kept[...] = pair
+        pair.wait_recv()
+        if dy == 1:
+            mate[t, 0] = (mine[t, 0].astype(F32) + mate[t, 0].astype(F32)).astype(BF)
+            start(mate.at[t, 0], from_y.at[dx], sy.at[dx], ry.at[dx], across)
         else:
-            mate[t] = pair.astype(BF)
-            copy = remote(mate.at[t], chip.at[j - 1], s2.at[j], r2.at[j],
-                          ctx_of(x + jx, yl + jy, core), h)
-            copy.start()
-            second.append(copy)
-    out = pltpu.make_async_copy(kept, keep, local.at[0])
-    out.start()
-    for copy in second:
-        copy.wait_recv()
-    for copy in first + second:
+            hold[dx] = mine[t, 0].astype(F32) + mate[t, 0].astype(F32)
+        if dx == 0:
+            kept[1 - dy] = mine[t, 1].astype(F32) + mate[t, 1].astype(F32)
+        else:
+            mate[t, 1] = (mine[t, 1].astype(F32) + mate[t, 1].astype(F32)).astype(BF)
+            start(mate.at[t, 1], from_x.at[dx - 1, dy], sx.at[dx - 1, dy], rx.at[dx - 1, dy],
+                  along(dx))
+
+    for dx in far:
+        remote(from_y.at[dx], from_y.at[dx], sy.at[dx], ry.at[dx], across, h).wait_recv()
+        hold[dx] += from_y[dx].astype(F32)
+        if dx:
+            t = place(dx, 0)
+            mate[t, 0] = hold[dx].astype(BF)
+            start(mate.at[t, 0], chip.at[dx - 1], s2.at[dx], r2.at[dx], along(dx))
+    for dy in (1, 0):
+        for dx in (1, 3, 2):
+            part_in = from_x.at[dx - 1, dy]
+            remote(part_in, part_in, sx.at[dx - 1, dy], rx.at[dx - 1, dy], across, h).wait_recv()
+            kept[1 - dy] += from_x[dx - 1, dy].astype(F32)
+        if dy:
+            t = place(0, 1)
+            mate[t, 1] = kept[0].astype(BF)
+            start(mate.at[t, 1], chip.at[3], s2.at[0], r2.at[0], across)
+    outs = [
+        pltpu.make_async_copy(hold.at[0], keep.at[0], local.at[0]),
+        pltpu.make_async_copy(kept.at[1], keep.at[1], local.at[1]),
+    ]
+    for out in outs:
+        out.start()
+    for j in range(4):
+        slot = chip.at[(j + 3) % 4]
+        remote(slot, slot, s2.at[j], r2.at[j], across, h).wait_recv()
+    for copy in sent:
         copy.wait_send()
-    out.wait()
+    for out in outs:
+        out.wait()
 
 
 def reduce(part):
-    shape = (2, SHARDS, BLOCK, HD)
+    shape = (SHARDS, BLOCK, HD)
     return pl.pallas_call(
         reduce_kernel,
         name="reduce",
         out_shape=(
-            jax.ShapeDtypeStruct((7,) + shape, BF),
-            jax.ShapeDtypeStruct(shape, F32),
+            jax.ShapeDtypeStruct((4,) + shape, BF),
+            jax.ShapeDtypeStruct((2,) + shape, F32),
         ),
         in_specs=[ANY],
         out_specs=(ANY, ANY),
         scratch_shapes=[
-            pltpu.VMEM((8,) + shape, BF),
-            pltpu.VMEM((8,) + shape, BF),
-            pltpu.VMEM(shape, F32),
+            pltpu.VMEM((8, 2) + shape, BF),
+            pltpu.VMEM((8, 2) + shape, BF),
+            pltpu.VMEM((4,) + shape, F32),
+            pltpu.VMEM((2,) + shape, F32),
+            pltpu.VMEM((4,) + shape, BF),
+            pltpu.VMEM((3, 2) + shape, BF),
             pltpu.SemaphoreType.DMA((8,)),
             pltpu.SemaphoreType.DMA((8,)),
-            pltpu.SemaphoreType.DMA((8,)),
-            pltpu.SemaphoreType.DMA((8,)),
+            pltpu.SemaphoreType.DMA((4,)),
+            pltpu.SemaphoreType.DMA((4,)),
+            pltpu.SemaphoreType.DMA((3, 2)),
+            pltpu.SemaphoreType.DMA((3, 2)),
+            pltpu.SemaphoreType.DMA((4,)),
+            pltpu.SemaphoreType.DMA((4,)),
             pltpu.SemaphoreType.DMA((8,)),
         ],
         compiler_params=pltpu.CompilerParams(collective_id=1, has_side_effects=True),
@@ -557,15 +605,12 @@
 
 
 def finish_kernel(chip, keep, dk, dv):
-    for a, out in enumerate((dk, dv)):
-        def add(s, carry):
-            total = keep[a, s]
-            for j in range(7):
-                total = total + chip[j, a, s].astype(F32)
-            out[s] = total
-            return carry
-
-        lax.fori_loop(0, SHARDS, add, 0)
+    def add(s, carry):
+        dk[s] = keep[0, s] + chip[0, s].astype(F32) + chip[1, s].astype(F32) + chip[2, s].astype(F32)
+        dv[s] = keep[1, s] + chip[3, s].astype(F32)
+        return carry
+
+    lax.fori_loop(0, SHARDS, add, 0)
 
 
 def finish(chip, keep):

time: 90.8 us -> 77.1 us (0.85)
  Pallas kernels: 89.9 us -> 76.2 us
    pallas_call x1, Pallas kernels: 26.6 us -> 18.5 us  [attention(): pl.pallas_call(attention_kernel, name='attention', out_shape=(jax.ShapeDt...]
    pallas_call x1, Pallas kernels: 20.3 us -> 15.1 us  [reduce(): pl.pallas_call(reduce_kernel, name='reduce', out_shape=(jax.ShapeDtypeStr...]
where the time goes in v3:
time: 77.1 us; the launch traced here: 76.9 us
  Pallas kernels  76.2 us (99%)
    pallas_call x1, Pallas kernels, exchange(): pl.pallas_call(exchange_kernel, name='exchange', out_shape=(jax.ShapeDtyp...  40.8 us
    pallas_call x1, Pallas kernels, attention(): pl.pallas_call(attention_kernel, name='attention', out_shape=(jax.ShapeDt...  18.5 us
    pallas_call x1, Pallas kernels, reduce(): pl.pallas_call(reduce_kernel, name='reduce', out_shape=(jax.ShapeDtypeStr...  15.1 us
    pallas_call x1, Pallas kernels, finish(): pl.pallas_call(finish_kernel, name='finish', out_shape=(out, out), in_spe...  1.85 us

profile of v3, /device:TPU:1, one launch (start us, length us, event | category | flops | bytes accessed | tf_op | source)
XLA Modules:
  0.0 76.9 jit_solution(5826079447329801830)
XLA Ops:
  0.6 40.8 %exchange.1 = (bf16[16,16,1024]{2,1,0:T(8,128)(2,1)}, bf16[16,16,1024]{2,1,0:T(8,128)(2,1)}, bf16[4096,128]{1,0:T(8,128)(2,1)}, bf16[4096,128]{1,0:T(8,128)(2,1)}) custom-call(s32[16,16]{1,0:T(8,128)} %route.3, bf16[2,16,8192]{2,1,0:T(8,128)(2,1)} %bitcast.10, bf16[32,1024]{1,0:T(8,128)(2,1)} %k.1, bf16[32,1024]{1,0:T(8,128)(2,1)} %v.1, ...), custom_call_target="tpu_custom_call" | custom-call | tf_op jit(solution)/shard_map/exchange/pallas_call | solution.py:224
  41.4 18.5 %attention.1 = (bf16[16,16,1024]{2,1,0:T(8,128)(2,1)}, f32[16,16,1024]{2,1,0:T(8,128)}, bf16[16,2,16,16,128]{4,3,2,1,0:T(8,128)(2,1)}) custom-call(s32[16,16]{1,0:T(8,128)} %route.3, s32[8]{0:T(128)} %docs.1, bf16[16,16,1024]{2,1,0:T(8,128)(2,1)} %get-tuple-element.15.q_hbm, bf16[16,16,1024]{2,1,0:T(8,128)(2,1)} %get-tuple-element.16.g_hbm, ...), custom_call_target="tpu_custom_call" | custom-call | tf_op jit(solution)/shard_map/attention/pallas_call | solution.py:453
  59.9 15.1 %reduce.1 = (bf16[4,16,16,128]{3,2,1,0:T(8,128)(2,1)}, f32[2,16,16,128]{3,2,1,0:T(8,128)}) custom-call(bf16[16,2,16,16,128]{4,3,2,1,0:T(8,128)(2,1)} %get-tuple-element.21.part), custom_call_target="tpu_custom_call" | custom-call | tf_op jit(solution)/shard_map/reduce/pallas_call | solution.py:577
  75.0 1.8 %finish.1 = (f32[16,16,128]{2,1,0:T(8,128)}, f32[16,16,128]{2,1,0:T(8,128)}) custom-call(bf16[4,16,16,128]{3,2,1,0:T(8,128)(2,1)} %get-tuple-element.22.chip, f32[2,16,16,128]{3,2,1,0:T(8,128)} %get-tuple-element.23.keep), custom_call_target="tpu_custom_call" | custom-call | tf_op jit(solution)/shard_map/finish/pallas_call | solution.py:618

commit v4 on v3

--- a/solution.py
+++ b/solution.py
@@ -254,16 +254,20 @@
 def attention_kernel(
     route, docs, q_hbm, g_hbm, k_hbm, v_hbm, att_hbm, dq_hbm, dkv_hbm,
     q, g, k, v, att, dq, dkv,
-    s_buf, kt, vt, dk_acc, dv_acc, ot_acc, dqt_acc, starts, load, store,
+    s_buf, dp_buf, kt, vt, dk_acc, dv_acc, ot_acc, dqt_acc, starts, load, store,
 ):
-    loads = [
-        pltpu.make_async_copy(k_hbm, k, load.at[0]),
-        pltpu.make_async_copy(v_hbm, v, load.at[1]),
-        pltpu.make_async_copy(q_hbm, q, load.at[2]),
-        pltpu.make_async_copy(g_hbm, g, load.at[3]),
-    ]
-    for copy in loads:
-        copy.start()
+    pairs = ((k_hbm, k), (q_hbm, q), (v_hbm, v), (g_hbm, g))
+
+    def incoming(n):
+        rows = pl.ds(n * SPAN, SPAN)
+        return [
+            pltpu.make_async_copy(src.at[rows], dst.at[rows], load.at[n, i])
+            for i, (src, dst) in enumerate(pairs)
+        ]
+
+    for n in range(SHARDS // SPAN):
+        for copy in incoming(n):
+            copy.start()
     c = lax.axis_index("ctx")
     ends = []
     total = jnp.int32(0)
@@ -279,18 +283,6 @@
         return carry
 
     lax.fori_loop(0, SHARDS, find, 0)
-    loads[0].wait()
-    loads[1].wait()
-
-    def prepare(t, carry):
-        kt[t] = k[t].T
-        vt[t] = v[t].T
-        return carry
-
-    lax.fori_loop(0, SHARDS, prepare, 0)
-    loads[2].wait()
-    loads[3].wait()
-
     def stack(ref, first):
         parts = []
         for i in range(SPAN):
@@ -310,6 +302,11 @@
 
     def group(n, carry):
         first = n * SPAN
+        for copy in incoming(n):
+            copy.wait()
+        for e in range(SPAN):
+            kt[first + e] = k[first + e].T
+            vt[first + e] = v[first + e].T
         qg = stack(q, first)
         gg = stack(g, first)
         qt = qg.T
@@ -330,6 +327,9 @@
             s = jnp.dot(k[t], qt[:, lane:stop], preferred_element_type=F32)
             return s * (SCALE * LOG2E)
 
+        def slopes(t, lane, stop=LANES):
+            return jnp.dot(v[t], gt[:, lane:stop], preferred_element_type=F32)
+
         def masked(t, lane, stop=LANES):
             s = scores(t, lane, stop)
             offset = t * ROWS - q_doc[:, lane:stop]
@@ -348,6 +348,8 @@
                 peak, mass = carried
                 s = produce(t, 0, stop)
                 s_buf[t, :, :stop] = s
+                if stop < LANES:
+                    dp_buf[t, :, :stop] = slopes(t, 0, stop)
                 new_peak = jnp.maximum(peak[:, :stop], jnp.max(s, axis=0, keepdims=True))
                 p = jnp.exp2(s - new_peak)
                 fade = jnp.exp2(peak[:, :stop] - new_peak)
@@ -371,6 +373,7 @@
         for e in range(SPAN):
             s = masked(first + e, e * WIDTH)
             s_buf[first + e, :, e * WIDTH:] = s
+            dp_buf[first + e, :, e * WIDTH:] = slopes(first + e, e * WIDTH)
             top = jnp.max(s, axis=0, keepdims=True)
             for i in range(e, SPAN):
                 tops[i].append(top[:, (i - e) * WIDTH:(i - e + 1) * WIDTH])
@@ -396,9 +399,9 @@
                 r = (i * GROUP + m) * BLOCK
                 att[first + i, :, m * HD:(m + 1) * HD] = o[r:r + BLOCK]
 
-        def pull(t, lane, stop=LANES):
+        def pull(t, lane, stop=LANES, held=True):
             p = jnp.exp2(s_buf[t, :, lane:stop] - lse[:, lane:stop])
-            dp = jnp.dot(v[t], gt[:, lane:stop], preferred_element_type=F32)
+            dp = dp_buf[t, :, lane:stop] if held else slopes(t, lane, stop)
             ds = (p * (dp - delta[:, lane:stop])).astype(BF)
             grad_v = jnp.dot(p.astype(BF), gg[lane:stop], preferred_element_type=F32)
             grad_k = jnp.dot(ds, qg[lane:stop], preferred_element_type=F32)
@@ -412,7 +415,7 @@
 
         def backward(stop):
             def step(t, carried):
-                grad_v, grad_k = pull(t, 0, stop)
+                grad_v, grad_k = pull(t, 0, stop, stop < LANES)
                 dv_acc[t] += grad_v
                 dk_acc[t] += grad_k
                 return carried
@@ -442,7 +445,7 @@
         return carry
 
     lax.fori_loop(0, SHARDS, regroup, 0)
-    last = pltpu.make_async_copy(dkv, dkv_hbm, load.at[0])
+    last = pltpu.make_async_copy(dkv, dkv_hbm, load.at[0, 0])
     last.start()
     pltpu.make_async_copy(att, att_hbm, store.at[0]).wait()
     pltpu.make_async_copy(dq, dq_hbm, store.at[1]).wait()
@@ -469,6 +472,7 @@
             pltpu.VMEM((SHARDS, BLOCK, COLS), F32),
             pltpu.VMEM((SHARDS, 2, SHARDS, BLOCK, HD), BF),
             pltpu.VMEM((SHARDS, ROWS, LANES), F32),
+            pltpu.VMEM((SHARDS, ROWS, LANES), F32),
             pltpu.VMEM((SHARDS, HD, ROWS), BF),
             pltpu.VMEM((SHARDS, HD, ROWS), BF),
             pltpu.VMEM((SHARDS, ROWS, HD), F32),
@@ -476,7 +480,7 @@
             pltpu.VMEM((HD, LANES), F32),
             pltpu.VMEM((HD, LANES), F32),
             pltpu.SMEM((SHARDS,), jnp.int32),
-            pltpu.SemaphoreType.DMA((4,)),
+            pltpu.SemaphoreType.DMA((SHARDS // SPAN, 4)),
             pltpu.SemaphoreType.DMA((2,)),
         ],
     )(route, docs, q, g, k, v)

time: 77.1 us -> 76.8 us (level)
    pallas_call x1, Pallas kernels: 18.5 us -> 15.4 us  [attention(): pl.pallas_call(attention_kernel, name='attention', out_shape=(jax.ShapeDt...]
    pallas_call x1, Pallas kernels: 15.1 us -> 18 us  [reduce(): pl.pallas_call(reduce_kernel, name='reduce', out_shape=(jax.ShapeDtypeStr...]
where the time goes in v4:
time: 76.8 us; the launch traced here: 76.6 us
  Pallas kernels  75.9 us (99%)
    pallas_call x1, Pallas kernels, exchange(): pl.pallas_call(exchange_kernel, name='exchange', out_shape=(jax.ShapeDtyp...  40.8 us
    pallas_call x1, Pallas kernels, reduce(): pl.pallas_call(reduce_kernel, name='reduce', out_shape=(jax.ShapeDtypeStr...  18 us
    pallas_call x1, Pallas kernels, attention(): pl.pallas_call(attention_kernel, name='attention', out_shape=(jax.ShapeDt...  15.4 us
    pallas_call x1, Pallas kernels, finish(): pl.pallas_call(finish_kernel, name='finish', out_shape=(out, out), in_spe...  1.85 us

profile of v4, /device:TPU:1, one launch (start us, length us, event | category | flops | bytes accessed | tf_op | source)
XLA Modules:
  0.0 76.6 jit_solution(17504894245631185025)
XLA Ops:
  0.6 40.8 %exchange.1 = (bf16[16,16,1024]{2,1,0:T(8,128)(2,1)}, bf16[16,16,1024]{2,1,0:T(8,128)(2,1)}, bf16[4096,128]{1,0:T(8,128)(2,1)}, bf16[4096,128]{1,0:T(8,128)(2,1)}) custom-call(s32[16,16]{1,0:T(8,128)} %route.3, bf16[2,16,8192]{2,1,0:T(8,128)(2,1)} %bitcast.10, bf16[32,1024]{1,0:T(8,128)(2,1)} %k.1, bf16[32,1024]{1,0:T(8,128)(2,1)} %v.1, ...), custom_call_target="tpu_custom_call" | custom-call | tf_op jit(solution)/shard_map/exchange/pallas_call | solution.py:224
  41.4 15.4 %attention.1 = (bf16[16,16,1024]{2,1,0:T(8,128)(2,1)}, f32[16,16,1024]{2,1,0:T(8,128)}, bf16[16,2,16,16,128]{4,3,2,1,0:T(8,128)(2,1)}) custom-call(s32[16,16]{1,0:T(8,128)} %route.3, s32[8]{0:T(128)} %docs.1, bf16[16,16,1024]{2,1,0:T(8,128)(2,1)} %get-tuple-element.15.q_hbm, bf16[16,16,1024]{2,1,0:T(8,128)(2,1)} %get-tuple-element.16.g_hbm, ...), custom_call_target="tpu_custom_call" | custom-call | tf_op jit(solution)/shard_map/attention/pallas_call | solution.py:456
  56.8 18.0 %reduce.1 = (bf16[4,16,16,128]{3,2,1,0:T(8,128)(2,1)}, f32[2,16,16,128]{3,2,1,0:T(8,128)}) custom-call(bf16[16,2,16,16,128]{4,3,2,1,0:T(8,128)(2,1)} %get-tuple-element.21.part), custom_call_target="tpu_custom_call" | custom-call | tf_op jit(solution)/shard_map/reduce/pallas_call | solution.py:581
  74.8 1.8 %finish.1 = (f32[16,16,128]{2,1,0:T(8,128)}, f32[16,16,128]{2,1,0:T(8,128)}) custom-call(bf16[4,16,16,128]{3,2,1,0:T(8,128)(2,1)} %get-tuple-element.22.chip, f32[2,16,16,128]{3,2,1,0:T(8,128)} %get-tuple-element.23.keep), custom_call_target="tpu_custom_call" | custom-call | tf_op jit(solution)/shard_map/finish/pallas_call | solution.py:622

commit v5 on v4

--- a/solution.py
+++ b/solution.py
@@ -54,7 +54,7 @@
 
 
 def exchange_kernel(
-    route, q, k, v, g, qo, go, ko, vo, xq, xg, sq, sg,
+    route_hbm, q, k, v, g, qo, go, ko, vo, xq, xg, sq, sg, own_kv, route,
     p1s, p1r, p2s, p2r, rs, rr, cs, cr, local,
 ):
     c = lax.axis_index("ctx")
@@ -67,6 +67,16 @@
         if (jx, jy, jc) != (0, 0, 0)
     ]
 
+    table = pltpu.make_async_copy(route_hbm, route, local.at[6])
+    table.start()
+    own_cols = pl.ds(pl.multiple_of(h * HD, HD), HD)
+    staged = [
+        pltpu.make_async_copy(src.at[:, own_cols], own_kv.at[a], local.at[a])
+        for a, src in enumerate((k, v))
+    ]
+    for copy in staged:
+        copy.start()
+
     barrier = pltpu.get_barrier_semaphore()
     for jz, jy in head_peers:
         pl.semaphore_signal(
@@ -94,10 +104,9 @@
         for a, (src, dst) in enumerate(((k, ko), (v, vo))):
             p1[a].append(go_remote(remote(
                 src.at[:, cols], dst.at[kv_rows], p1s.at[a, j], p1r.at[a, j], c, peer)))
-    own_cols = pl.ds(pl.multiple_of(h * HD, HD), HD)
     own = [
-        pltpu.make_async_copy(k.at[:, own_cols], ko.at[kv_rows], local.at[0]),
-        pltpu.make_async_copy(v.at[:, own_cols], vo.at[kv_rows], local.at[1]),
+        pltpu.make_async_copy(own_kv.at[a], dst.at[kv_rows], local.at[a])
+        for a, dst in enumerate((ko, vo))
     ]
 
     def first(a, src, dst):
@@ -113,9 +122,10 @@
             src.at[:, :, cols], dst.at[pl.ds(h * 2, 2)], local.at[2 + a]))
         own[-1].start()
 
-    for copy in own:
-        copy.start()
     first(0, q, xq)
+    for a in range(2):
+        staged[a].wait()
+        own[a].start()
 
     kv = (ko, vo)
 
@@ -149,6 +159,8 @@
     first(1, g, xg)
     for a in range(2):
         go_remote(partner(a, 0, 0))
+
+    table.wait()
 
     def second(a, stage, send, out):
         own[2 + a].wait()
@@ -230,13 +242,15 @@
             jax.ShapeDtypeStruct((SEQ, HD), BF),
             jax.ShapeDtypeStruct((SEQ, HD), BF),
         ),
-        in_specs=[SMEM, ANY, VMEM, VMEM, ANY],
+        in_specs=[ANY, ANY, ANY, ANY, ANY],
         out_specs=(ANY, ANY, ANY, ANY),
         scratch_shapes=[
             pltpu.VMEM((SHARDS, BLOCK, COLS), BF),
             pltpu.VMEM((SHARDS, BLOCK, COLS), BF),
             pltpu.VMEM((SHARDS, BLOCK, COLS), BF),
             pltpu.VMEM((SHARDS, BLOCK, COLS), BF),
+            pltpu.VMEM((2, 32, HD), BF),
+            pltpu.SMEM((SHARDS, SHARDS), jnp.int32),
             pltpu.SemaphoreType.DMA((4, 8)),
             pltpu.SemaphoreType.DMA((4, 8)),
             pltpu.SemaphoreType.DMA((2, 16)),
@@ -245,17 +259,23 @@
             pltpu.SemaphoreType.DMA((2, 8)),
             pltpu.SemaphoreType.DMA((2, 8)),
             pltpu.SemaphoreType.DMA((2, 8)),
-            pltpu.SemaphoreType.DMA((6,)),
+            pltpu.SemaphoreType.DMA((7,)),
         ],
         compiler_params=pltpu.CompilerParams(collective_id=0, has_side_effects=True),
     )(route, q, k, v, g)
 
 
 def attention_kernel(
-    route, docs, q_hbm, g_hbm, k_hbm, v_hbm, att_hbm, dq_hbm, dkv_hbm,
+    route_hbm, docs_hbm, q_hbm, g_hbm, k_hbm, v_hbm, att_hbm, dq_hbm, dkv_hbm,
     q, g, k, v, att, dq, dkv,
-    s_buf, dp_buf, kt, vt, dk_acc, dv_acc, ot_acc, dqt_acc, starts, load, store,
+    s_buf, dp_buf, kt, vt, dk_acc, dv_acc, ot_acc, dqt_acc, route, docs, starts, load, store,
 ):
+    tables = (
+        pltpu.make_async_copy(route_hbm, route, store.at[0]),
+        pltpu.make_async_copy(docs_hbm, docs, store.at[1]),
+    )
+    for copy in tables:
+        copy.start()
     pairs = ((k_hbm, k), (q_hbm, q), (v_hbm, v), (g_hbm, g))
 
     def incoming(n):
@@ -268,6 +288,8 @@
     for n in range(SHARDS // SPAN):
         for copy in incoming(n):
             copy.start()
+    for copy in tables:
+        copy.wait()
     c = lax.axis_index("ctx")
     ends = []
     total = jnp.int32(0)
@@ -436,20 +458,24 @@
 
     lax.fori_loop(0, SHARDS // SPAN, group, 0)
 
+    def outbound(n):
+        cols = pl.ds(n * SPAN, SPAN)
+        return pltpu.make_async_copy(dkv.at[:, cols], dkv_hbm.at[:, cols], load.at[n, 0])
+
     def regroup(s, carry):
         for b in range(SHARDS):
-            d = route[s, b]
             rows = slice(b * BLOCK, (b + 1) * BLOCK)
-            dkv[d, 0, s] = (dk_acc[s, rows] * SCALE).astype(BF)
-            dkv[d, 1, s] = dv_acc[s, rows].astype(BF)
+            dkv[route[s, b], s] = jnp.stack(
+                [(dk_acc[s, rows] * SCALE).astype(BF), dv_acc[s, rows].astype(BF)])
         return carry
 
-    lax.fori_loop(0, SHARDS, regroup, 0)
-    last = pltpu.make_async_copy(dkv, dkv_hbm, load.at[0, 0])
-    last.start()
+    for n in range(SHARDS // SPAN):
+        lax.fori_loop(n * SPAN, (n + 1) * SPAN, regroup, 0)
+        outbound(n).start()
     pltpu.make_async_copy(att, att_hbm, store.at[0]).wait()
     pltpu.make_async_copy(dq, dq_hbm, store.at[1]).wait()
-    last.wait()
+    for n in range(SHARDS // SPAN):
+        outbound(n).wait()
 
 
 def attention(route, docs, q, g, k, v):
@@ -459,9 +485,9 @@
         out_shape=(
             jax.ShapeDtypeStruct((SHARDS, BLOCK, COLS), BF),
             jax.ShapeDtypeStruct((SHARDS, BLOCK, COLS), F32),
-            jax.ShapeDtypeStruct((SHARDS, 2, SHARDS, BLOCK, HD), BF),
+            jax.ShapeDtypeStruct((SHARDS, SHARDS, 2, BLOCK, HD), BF),
         ),
-        in_specs=[SMEM, SMEM, ANY, ANY, ANY, ANY],
+        in_specs=[ANY, ANY, ANY, ANY, ANY, ANY],
         out_specs=(ANY, ANY, ANY),
         scratch_shapes=[
             pltpu.VMEM((SHARDS, BLOCK, COLS), BF),
@@ -470,7 +496,7 @@
             pltpu.VMEM((SHARDS, ROWS, HD), BF),
             pltpu.VMEM((SHARDS, BLOCK, COLS), BF),
             pltpu.VMEM((SHARDS, BLOCK, COLS), F32),
-            pltpu.VMEM((SHARDS, 2, SHARDS, BLOCK, HD), BF),
+            pltpu.VMEM((SHARDS, SHARDS, 2, BLOCK, HD), BF),
             pltpu.VMEM((SHARDS, ROWS, LANES), F32),
             pltpu.VMEM((SHARDS, ROWS, LANES), F32),
             pltpu.VMEM((SHARDS, HD, ROWS), BF),
@@ -479,6 +505,8 @@
             pltpu.VMEM((SHARDS, ROWS, HD), F32),
             pltpu.VMEM((HD, LANES), F32),
             pltpu.VMEM((HD, LANES), F32),
+            pltpu.SMEM((SHARDS, SHARDS), jnp.int32),
+            pltpu.SMEM((DOCS,), jnp.int32),
             pltpu.SMEM((SHARDS,), jnp.int32),
             pltpu.SemaphoreType.DMA((SHARDS // SPAN, 4)),
             pltpu.SemaphoreType.DMA((2,)),
@@ -487,7 +515,7 @@
 
 
 def reduce_kernel(
-    part, chip, keep, mine, mate, hold, kept, from_y, from_x,
+    part, chip, keep, mine, mate, ready, hold, kept, from_y, from_x,
     s1, r1, sy, ry, sx, rx, s2, r2, local,
 ):
     c = lax.axis_index("ctx")
@@ -533,16 +561,17 @@
         t = place(dx, dy)
         load.wait()
         pair.wait_recv()
+        sums = [mine[t, :, a].astype(F32) + mate[t, :, a].astype(F32) for a in range(2)]
         if dy == 1:
-            mate[t, 0] = (mine[t, 0].astype(F32) + mate[t, 0].astype(F32)).astype(BF)
-            start(mate.at[t, 0], from_y.at[dx], sy.at[dx], ry.at[dx], across)
+            ready[t, 0] = sums[0].astype(BF)
+            start(ready.at[t, 0], from_y.at[dx], sy.at[dx], ry.at[dx], across)
         else:
-            hold[dx] = mine[t, 0].astype(F32) + mate[t, 0].astype(F32)
+            hold[dx] = sums[0]
         if dx == 0:
-            kept[1 - dy] = mine[t, 1].astype(F32) + mate[t, 1].astype(F32)
+            kept[1 - dy] = sums[1]
         else:
-            mate[t, 1] = (mine[t, 1].astype(F32) + mate[t, 1].astype(F32)).astype(BF)
-            start(mate.at[t, 1], from_x.at[dx - 1, dy], sx.at[dx - 1, dy], rx.at[dx - 1, dy],
+            ready[t, 1] = sums[1].astype(BF)
+            start(ready.at[t, 1], from_x.at[dx - 1, dy], sx.at[dx - 1, dy], rx.at[dx - 1, dy],
                   along(dx))
 
     for dx in far:
@@ -550,8 +579,8 @@
         hold[dx] += from_y[dx].astype(F32)
         if dx:
             t = place(dx, 0)
-            mate[t, 0] = hold[dx].astype(BF)
-            start(mate.at[t, 0], chip.at[dx - 1], s2.at[dx], r2.at[dx], along(dx))
+            ready[t, 0] = hold[dx].astype(BF)
+            start(ready.at[t, 0], chip.at[dx - 1], s2.at[dx], r2.at[dx], along(dx))
     for dy in (1, 0):
         for dx in (1, 3, 2):
             part_in = from_x.at[dx - 1, dy]
@@ -559,8 +588,8 @@
             kept[1 - dy] += from_x[dx - 1, dy].astype(F32)
         if dy:
             t = place(0, 1)
-            mate[t, 1] = kept[0].astype(BF)
-            start(mate.at[t, 1], chip.at[3], s2.at[0], r2.at[0], across)
+            ready[t, 1] = kept[0].astype(BF)
+            start(ready.at[t, 1], chip.at[3], s2.at[0], r2.at[0], across)
     outs = [
         pltpu.make_async_copy(hold.at[0], keep.at[0], local.at[0]),
         pltpu.make_async_copy(kept.at[1], keep.at[1], local.at[1]),
@@ -588,7 +617,8 @@
         in_specs=[ANY],
         out_specs=(ANY, ANY),
         scratch_shapes=[
-            pltpu.VMEM((8, 2) + shape, BF),
+            pltpu.VMEM((8, SHARDS, 2, BLOCK, HD), BF),
+            pltpu.VMEM((8, SHARDS, 2, BLOCK, HD), BF),
             pltpu.VMEM((8, 2) + shape, BF),
             pltpu.VMEM((4,) + shape, F32),
             pltpu.VMEM((2,) + shape, F32),

time: 76.8 us -> 75.8 us (0.987)
  Pallas kernels: 75.9 us -> 75 us
    pallas_call x1, Pallas kernels: 18 us -> 15.1 us  [reduce(): pl.pallas_call(reduce_kernel, name='reduce', out_shape=(jax.ShapeDtypeStr...]
    pallas_call x1, Pallas kernels: 15.4 us -> 17.9 us  [attention(): pl.pallas_call(attention_kernel, name='attention', out_shape=(jax.ShapeDt...]
where the time goes in v5:
time: 75.8 us; the launch traced here: 75.7 us
  Pallas kernels  75 us (99%)
    pallas_call x1, Pallas kernels, exchange(): pl.pallas_call(exchange_kernel, name='exchange', out_shape=(jax.ShapeDtyp...  40.1 us
    pallas_call x1, Pallas kernels, attention(): pl.pallas_call(attention_kernel, name='attention', out_shape=(jax.ShapeDt...  17.9 us
    pallas_call x1, Pallas kernels, reduce(): pl.pallas_call(reduce_kernel, name='reduce', out_shape=(jax.ShapeDtypeStr...  15.1 us
    pallas_call x1, Pallas kernels, finish(): pl.pallas_call(finish_kernel, name='finish', out_shape=(out, out), in_spe...  1.85 us

profile of v5, /device:TPU:1, one launch (start us, length us, event | category | flops | bytes accessed | tf_op | source)
XLA Modules:
  0.0 75.7 jit_solution(12192106170775911063)
XLA Ops:
  0.6 40.1 %exchange.1 = (bf16[16,16,1024]{2,1,0:T(8,128)(2,1)}, bf16[16,16,1024]{2,1,0:T(8,128)(2,1)}, bf16[4096,128]{1,0:T(8,128)(2,1)}, bf16[4096,128]{1,0:T(8,128)(2,1)}) custom-call(s32[16,16]{1,0:T(8,128)} %route_hbm.3, bf16[2,16,8192]{2,1,0:T(8,128)(2,1)} %bitcast.10, bf16[32,1024]{1,0:T(8,128)(2,1)} %k.1, bf16[32,1024]{1,0:T(8,128)(2,1)} %v.1, ...), custom_call_target="tpu_custom_call" | custom-call | tf_op jit(solution)/shard_map/exchange/pallas_call | solution.py:236
  40.8 17.9 %attention.1 = (bf16[16,16,1024]{2,1,0:T(8,128)(2,1)}, f32[16,16,1024]{2,1,0:T(8,128)}, bf16[16,16,2,16,128]{4,3,2,1,0:T(8,128)(2,1)}) custom-call(s32[16,16]{1,0:T(8,128)} %route_hbm.3, s32[8]{0:T(128)} %docs_hbm.1, bf16[16,16,1024]{2,1,0:T(8,128)(2,1)} %get-tuple-element.15.q_hbm, bf16[16,16,1024]{2,1,0:T(8,128)(2,1)} %get-tuple-element.16.g_hbm, ...), custom_call_target="tpu_custom_call" | custom-call | tf_op jit(solution)/shard_map/attention/pallas_call | solution.py:482
  58.7 15.1 %reduce.1 = (bf16[4,16,16,128]{3,2,1,0:T(8,128)(2,1)}, f32[2,16,16,128]{3,2,1,0:T(8,128)}) custom-call(bf16[16,16,2,16,128]{4,3,2,1,0:T(8,128)(2,1)} %get-tuple-element.21.part), custom_call_target="tpu_custom_call" | custom-call | tf_op jit(solution)/shard_map/reduce/pallas_call | solution.py:610
  73.8 1.8 %finish.1 = (f32[16,16,128]{2,1,0:T(8,128)}, f32[16,16,128]{2,1,0:T(8,128)}) custom-call(bf16[4,16,16,128]{3,2,1,0:T(8,128)(2,1)} %get-tuple-element.22.chip, f32[2,16,16,128]{3,2,1,0:T(8,128)} %get-tuple-element.23.keep), custom_call_target="tpu_custom_call" | custom-call | tf_op jit(solution)/shard_map/finish/pallas_call | solution.py:652

commit v6 on v5

--- a/solution.py
+++ b/solution.py
@@ -54,7 +54,8 @@
 
 
 def exchange_kernel(
-    route_hbm, q, k, v, g, qo, go, ko, vo, xq, xg, sq, sg, own_kv, route,
+    route_hbm, q, k, v, g, qo, go, ko, vo, kto, vto,
+    xq, xg, sq, sg, own_kv, all_kv, turned, route,
     p1s, p1r, p2s, p2r, rs, rr, cs, cr, local,
 ):
     c = lax.axis_index("ctx")
@@ -211,6 +212,28 @@
     for a in range(2):
         arrived(a, 2, 1)
         go_remote(partner(a, 2, 1))
+    for a in range(2):
+        for dx in range(4):
+            for dy in range(2):
+                slot = dx * 2 + dy
+                part = kv[a].at[pl.ds(ctx_of(x + dx, yl + dy, core + 1) * ROWS, ROWS)]
+                remote(part, part, cs.at[a, slot], cr.at[a, slot], c, h).wait_recv()
+    fetch = [pltpu.make_async_copy(kv[a], all_kv.at[a], local.at[a]) for a in range(2)]
+    for copy in fetch:
+        copy.start()
+    turns = []
+    for a, out in enumerate((kto, vto)):
+        fetch[a].wait()
+
+        def turn(i, carry):
+            for e in range(4):
+                t = i * 4 + e
+                turned[a, t] = all_kv[a, pl.ds(pl.multiple_of(t * ROWS, ROWS), ROWS), :].T
+            return carry
+
+        lax.fori_loop(0, SHARDS // 4, turn, 0)
+        turns.append(pltpu.make_async_copy(turned.at[a], out, local.at[2 + a]))
+        turns[-1].start()
     mine_q.wait()
     mine_g.wait()
 
@@ -221,13 +244,9 @@
             remote(out.at[src], out.at[src], p2s.at[a, j], p2r.at[a, j], c, h).wait_recv()
 
     received(0, qo)
+    for copy in turns:
+        copy.wait()
     received(1, go)
-    for a in range(2):
-        for dx in range(4):
-            for dy in range(2):
-                slot = dx * 2 + dy
-                part = kv[a].at[pl.ds(ctx_of(x + dx, yl + dy, core + 1) * ROWS, ROWS)]
-                remote(part, part, cs.at[a, slot], cr.at[a, slot], c, h).wait_recv()
     for copy in sent:
         copy.wait_send()
 
@@ -241,15 +260,19 @@
             jax.ShapeDtypeStruct((SHARDS, BLOCK, COLS), BF),
             jax.ShapeDtypeStruct((SEQ, HD), BF),
             jax.ShapeDtypeStruct((SEQ, HD), BF),
+            jax.ShapeDtypeStruct((SHARDS, HD, ROWS), BF),
+            jax.ShapeDtypeStruct((SHARDS, HD, ROWS), BF),
         ),
         in_specs=[ANY, ANY, ANY, ANY, ANY],
-        out_specs=(ANY, ANY, ANY, ANY),
+        out_specs=(ANY,) * 6,
         scratch_shapes=[
             pltpu.VMEM((SHARDS, BLOCK, COLS), BF),
             pltpu.VMEM((SHARDS, BLOCK, COLS), BF),
             pltpu.VMEM((SHARDS, BLOCK, COLS), BF),
             pltpu.VMEM((SHARDS, BLOCK, COLS), BF),
             pltpu.VMEM((2, 32, HD), BF),
+            pltpu.VMEM((2, SEQ, HD), BF),
+            pltpu.VMEM((2, SHARDS, HD, ROWS), BF),
             pltpu.SMEM((SHARDS, SHARDS), jnp.int32),
             pltpu.SemaphoreType.DMA((4, 8)),
             pltpu.SemaphoreType.DMA((4, 8)),
@@ -266,7 +289,7 @@
 
 
 def attention_kernel(
-    route_hbm, docs_hbm, q_hbm, g_hbm, k_hbm, v_hbm, att_hbm, dq_hbm, dkv_hbm,
+    route_hbm, docs_hbm, q_hbm, g_hbm, k_hbm, v_hbm, kt_hbm, vt_hbm, att_hbm, dq_hbm, dkv_hbm,
     q, g, k, v, att, dq, dkv,
     s_buf, dp_buf, kt, vt, dk_acc, dv_acc, ot_acc, dqt_acc, route, docs, starts, load, store,
 ):
@@ -276,7 +299,7 @@
     )
     for copy in tables:
         copy.start()
-    pairs = ((k_hbm, k), (q_hbm, q), (v_hbm, v), (g_hbm, g))
+    pairs = ((k_hbm, k), (q_hbm, q), (v_hbm, v), (g_hbm, g), (vt_hbm, vt), (kt_hbm, kt))
 
     def incoming(n):
         rows = pl.ds(n * SPAN, SPAN)
@@ -326,23 +349,20 @@
         first = n * SPAN
         for copy in incoming(n):
             copy.wait()
-        for e in range(SPAN):
-            kt[first + e] = k[first + e].T
-            vt[first + e] = v[first + e].T
         qg = stack(q, first)
         gg = stack(g, first)
         qt = qg.T
         gt = gg.T
         q_pos = jnp.concatenate([within + starts[first + i] for i in range(SPAN)], axis=1)
         q_doc = jnp.zeros_like(q_pos)
-        marks = [starts[first], starts[first + 1], starts[first + 2],
-                 starts[first + SPAN - 1] + BLOCK - 1]
-        lows = [jnp.int32(0)] * 4
+        marks = [starts[first], starts[first + 1], starts[first + 2]]
+        lows = [jnp.int32(0)] * 3
         for end in ends:
             q_doc = jnp.where(q_pos >= end, end, q_doc)
             lows = [jnp.where(mark >= end, end, low) for mark, low in zip(marks, lows)]
-        t_one, t_two, t_low = [jnp.minimum(low // ROWS, first) for low in lows[:3]]
-        t_full = jnp.minimum((lows[3] + ROWS - 1) // ROWS, first)
+        t_one, t_two, t_low = [jnp.minimum(low // ROWS, first) for low in lows]
+        t_even = t_low + lax.rem(first - t_low, 2)
+        twos = (first - t_even) // 2
         reach = (q_pos - q_doc).astype(jnp.uint32)
 
         def scores(t, lane, stop=LANES):
@@ -365,19 +385,25 @@
         ot_acc[...] = jnp.zeros_like(ot_acc)
         dqt_acc[...] = jnp.zeros_like(dqt_acc)
 
-        def forward(produce, stop=LANES):
-            def step(t, carried):
+        def forward(base, width, stop):
+            def step(n, carried):
                 peak, mass = carried
-                s = produce(t, 0, stop)
-                s_buf[t, :, :stop] = s
-                if stop < LANES:
-                    dp_buf[t, :, :stop] = slopes(t, 0, stop)
-                new_peak = jnp.maximum(peak[:, :stop], jnp.max(s, axis=0, keepdims=True))
-                p = jnp.exp2(s - new_peak)
+                tiles = [base + n * width + i for i in range(width)]
+                new_peak = peak[:, :stop]
+                for t in tiles:
+                    s = masked(t, 0, stop)
+                    s_buf[t, :, :stop] = s
+                    if stop < LANES or width == 2:
+                        dp_buf[t, :, :stop] = slopes(t, 0, stop)
+                    new_peak = jnp.maximum(new_peak, jnp.max(s, axis=0, keepdims=True))
                 fade = jnp.exp2(peak[:, :stop] - new_peak)
-                new_mass = mass[:, :stop] * fade + jnp.sum(p, axis=0, keepdims=True)
-                ot_acc[:, :stop] = ot_acc[:, :stop] * fade + jnp.dot(
-                    vt[t], p.astype(BF), preferred_element_type=F32)
+                new_mass = mass[:, :stop] * fade
+                total = ot_acc[:, :stop] * fade
+                for t in tiles:
+                    p = jnp.exp2(s_buf[t, :, :stop] - new_peak)
+                    new_mass = new_mass + jnp.sum(p, axis=0, keepdims=True)
+                    total = total + jnp.dot(vt[t], p.astype(BF), preferred_element_type=F32)
+                ot_acc[:, :stop] = total
                 if stop < LANES:
                     new_peak = jnp.concatenate([new_peak, peak[:, stop:]], axis=1)
                     new_mass = jnp.concatenate([new_mass, mass[:, stop:]], axis=1)
@@ -386,10 +412,10 @@
             return step
 
         state = (jnp.full((1, LANES), FLOOR, F32), jnp.zeros((1, LANES), F32))
-        state = lax.fori_loop(t_one, t_two, forward(masked, WIDTH), state)
-        state = lax.fori_loop(t_two, t_low, forward(masked, 2 * WIDTH), state)
-        state = lax.fori_loop(t_low, t_full, forward(masked), state)
-        peak, mass = lax.fori_loop(t_full, first, forward(scores), state)
+        state = lax.fori_loop(0, t_two - t_one, forward(t_one, 1, WIDTH), state)
+        state = lax.fori_loop(0, t_low - t_two, forward(t_two, 1, 2 * WIDTH), state)
+        state = lax.fori_loop(0, t_even - t_low, forward(t_low, 1, LANES), state)
+        peak, mass = lax.fori_loop(0, twos, forward(t_even, 2, LANES), state)
 
         tops = [[peak[:, i * WIDTH:(i + 1) * WIDTH]] for i in range(SPAN)]
         for e in range(SPAN):
@@ -435,18 +461,25 @@
             dv_acc[first + e] = grad_v
             dk_acc[first + e] = grad_k
 
-        def backward(stop):
+        def backward(stop, held):
             def step(t, carried):
-                grad_v, grad_k = pull(t, 0, stop, stop < LANES)
+                grad_v, grad_k = pull(t, 0, stop, held)
                 dv_acc[t] += grad_v
                 dk_acc[t] += grad_k
                 return carried
 
             return step
 
-        lax.fori_loop(t_one, t_two, backward(WIDTH), 0)
-        lax.fori_loop(t_two, t_low, backward(2 * WIDTH), 0)
-        lax.fori_loop(t_low, first, backward(LANES), 0)
+        lax.fori_loop(t_one, t_two, backward(WIDTH, True), 0)
+        lax.fori_loop(t_two, t_low, backward(2 * WIDTH, True), 0)
+        lax.fori_loop(t_low, t_even, backward(LANES, False), 0)
+
+        def backward_two(n, carried):
+            for i in range(2):
+                backward(LANES, True)(t_even + n * 2 + i, carried)
+            return carried
+
+        lax.fori_loop(0, twos, backward_two, 0)
         grad = dqt_acc[...].T * SCALE
         for i in range(SPAN):
             for m in range(GROUP):
@@ -478,7 +511,7 @@
         outbound(n).wait()
 
 
-def attention(route, docs, q, g, k, v):
+def attention(route, docs, q, g, k, v, kt, vt):
     return pl.pallas_call(
         attention_kernel,
         name="attention",
@@ -487,7 +520,7 @@
             jax.ShapeDtypeStruct((SHARDS, BLOCK, COLS), F32),
             jax.ShapeDtypeStruct((SHARDS, SHARDS, 2, BLOCK, HD), BF),
         ),
-        in_specs=[ANY, ANY, ANY, ANY, ANY, ANY],
+        in_specs=[ANY] * 8,
         out_specs=(ANY, ANY, ANY),
         scratch_shapes=[
             pltpu.VMEM((SHARDS, BLOCK, COLS), BF),
@@ -508,10 +541,10 @@
             pltpu.SMEM((SHARDS, SHARDS), jnp.int32),
             pltpu.SMEM((DOCS,), jnp.int32),
             pltpu.SMEM((SHARDS,), jnp.int32),
-            pltpu.SemaphoreType.DMA((SHARDS // SPAN, 4)),
+            pltpu.SemaphoreType.DMA((SHARDS // SPAN, 6)),
             pltpu.SemaphoreType.DMA((2,)),
         ],
-    )(route, docs, q, g, k, v)
+    )(route, docs, q, g, k, v, kt, vt)
 
 
 def reduce_kernel(
@@ -638,13 +671,28 @@
     )(part)
 
 
-def finish_kernel(chip, keep, dk, dv):
-    def add(s, carry):
-        dk[s] = keep[0, s] + chip[0, s].astype(F32) + chip[1, s].astype(F32) + chip[2, s].astype(F32)
-        dv[s] = keep[1, s] + chip[3, s].astype(F32)
-        return carry
-
-    lax.fori_loop(0, SHARDS, add, 0)
+def finish_kernel(chip_hbm, keep_hbm, dk_hbm, dv_hbm, chip, keep, load, store):
+    parts = (pl.ds(0, 3), pl.ds(3, 1))
+    loads = []
+    for a in range(2):
+        loads.append((
+            pltpu.make_async_copy(chip_hbm.at[parts[a]], chip.at[parts[a]], load.at[a, 0]),
+            pltpu.make_async_copy(keep_hbm.at[a], keep.at[a], load.at[a, 1]),
+        ))
+        for copy in loads[a]:
+            copy.start()
+    outs = []
+    for a, out in enumerate((dk_hbm, dv_hbm)):
+        for copy in loads[a]:
+            copy.wait()
+        total = keep[a]
+        for j in ((0, 1, 2), (3,))[a]:
+            total = total + chip[j].astype(F32)
+        keep[a] = total
+        outs.append(pltpu.make_async_copy(keep.at[a], out, store.at[a]))
+        outs[a].start()
+    for copy in outs:
+        copy.wait()
 
 
 def finish(chip, keep):
@@ -653,13 +701,19 @@
         finish_kernel,
         name="finish",
         out_shape=(out, out),
-        in_specs=[VMEM, VMEM],
-        out_specs=(VMEM, VMEM),
+        in_specs=[ANY, ANY],
+        out_specs=(ANY, ANY),
+        scratch_shapes=[
+            pltpu.VMEM(chip.shape, BF),
+            pltpu.VMEM(keep.shape, F32),
+            pltpu.SemaphoreType.DMA((2, 2)),
+            pltpu.SemaphoreType.DMA((2,)),
+        ],
     )(chip, keep)
 
 
 def on_device(queries, key_rows, value_rows, cotangent, doc_lengths, block_route):
-    q, g, k, v = exchange(
+    q, g, k, v, kt, vt = exchange(
         block_route,
         queries.reshape(2, BLOCK, HEADS * COLS),
         key_rows,
@@ -667,7 +721,7 @@
         cotangent.reshape(2, BLOCK, HEADS * COLS),
     )
     att, dq, part = attention(
-        block_route, doc_lengths, q, g, k.reshape(SHARDS, ROWS, HD), v.reshape(SHARDS, ROWS, HD))
+        block_route, doc_lengths, q, g, k.reshape(SHARDS, ROWS, HD), v.reshape(SHARDS, ROWS, HD), kt, vt)
     dk, dv = finish(*reduce(part))
     return (
         att.reshape(ROWS, COLS),

time: 75.8 us -> 75.2 us (level)
  Pallas kernels: 75 us -> 74 us
    pallas_call x1, Pallas kernels: 17.9 us -> 17.1 us  [attention(): pl.pallas_call(attention_kernel, name='attention', out_shape=(jax.ShapeDt...]
where the time goes in v6:
time: 75.2 us; the launch traced here: 74.6 us
  Pallas kernels  74 us (98%)
    pallas_call x1, Pallas kernels, exchange(): pl.pallas_call(exchange_kernel, name='exchange', out_shape=(jax.ShapeDtyp...  40.1 us
    pallas_call x1, Pallas kernels, attention(): pl.pallas_call(attention_kernel, name='attention', out_shape=(jax.ShapeDt...  17.1 us
    pallas_call x1, Pallas kernels, reduce(): pl.pallas_call(reduce_kernel, name='reduce', out_shape=(jax.ShapeDtypeStr...  15 us
    pallas_call x1, Pallas kernels, finish(): pl.pallas_call(finish_kernel, name='finish', out_shape=(out, out), in_spe...  1.81 us

profile of v6, /device:TPU:1, one launch (start us, length us, event | category | flops | bytes accessed | tf_op | source)
XLA Modules:
  0.0 74.6 jit_solution(4662705742818126781)
XLA Ops:
  0.6 40.1 %exchange.1 = (bf16[16,16,1024]{2,1,0:T(8,128)(2,1)}, bf16[16,16,1024]{2,1,0:T(8,128)(2,1)}, bf16[4096,128]{1,0:T(8,128)(2,1)}, bf16[4096,128]{1,0:T(8,128)(2,1)...) custom-call(s32[16,16]{1,0:T(8,128)} %route_hbm.3, bf16[2,16,8192]{2,1,0:T(8,128)(2,1)} %bitcast.10, ...), custom_call_target="tpu_custom_call" | custom-call | tf_op jit(solution)/shard_map/exchange/pallas_call | solution.py:255
  40.7 17.1 %attention.1 = (bf16[16,16,1024]{2,1,0:T(8,128)(2,1)}, f32[16,16,1024]{2,1,0:T(8,128)}, bf16[16,16,2,16,128]{4,3,2,1,0:T(8,128)(2,1)}) custom-call(s32[16,16]{1,0:T(8,128)} %route_hbm.3, s32[8]{0:T(128)} %docs_hbm.1, bf16[16,16,1024]{2,1,0:T(8,128)(2,1)} %get-tuple-element.17.q_hbm, bf16[16,16,1024]{2,1,0:T(8,128)(2,1)} %get-tuple-element.18.g_hbm, ...), custom_call_target="tpu_custom_call" | custom-call | tf_op jit(solution)/shard_map/attention/pallas_call | solution.py:515
  57.8 15.0 %reduce.1 = (bf16[4,16,16,128]{3,2,1,0:T(8,128)(2,1)}, f32[2,16,16,128]{3,2,1,0:T(8,128)}) custom-call(bf16[16,16,2,16,128]{4,3,2,1,0:T(8,128)(2,1)} %get-tuple-element.25.part), custom_call_target="tpu_custom_call" | custom-call | tf_op jit(solution)/shard_map/reduce/pallas_call | solution.py:643
  72.8 1.8 %finish.1 = (f32[16,16,128]{2,1,0:T(8,128)}, f32[16,16,128]{2,1,0:T(8,128)}) custom-call(bf16[4,16,16,128]{3,2,1,0:T(8,128)(2,1)} %get-tuple-element.26.chip_hbm, f32[2,16,16,128]{3,2,1,0:T(8,128)} %get-tuple-element.27.keep_hbm), custom_call_target="tpu_custom_call" | custom-call | tf_op jit(solution)/shard_map/finish/pallas_call | solution.py:700

commit v7 on v6

--- a/solution.py
+++ b/solution.py
@@ -361,8 +361,7 @@
             q_doc = jnp.where(q_pos >= end, end, q_doc)
             lows = [jnp.where(mark >= end, end, low) for mark, low in zip(marks, lows)]
         t_one, t_two, t_low = [jnp.minimum(low // ROWS, first) for low in lows]
-        t_even = t_low + lax.rem(first - t_low, 2)
-        twos = (first - t_even) // 2
+        spans = ((t_one, t_two, WIDTH), (t_two, t_low, 2 * WIDTH), (t_low, first, LANES))
         reach = (q_pos - q_doc).astype(jnp.uint32)
 
         def scores(t, lane, stop=LANES):
@@ -412,10 +411,11 @@
             return step
 
         state = (jnp.full((1, LANES), FLOOR, F32), jnp.zeros((1, LANES), F32))
-        state = lax.fori_loop(0, t_two - t_one, forward(t_one, 1, WIDTH), state)
-        state = lax.fori_loop(0, t_low - t_two, forward(t_two, 1, 2 * WIDTH), state)
-        state = lax.fori_loop(0, t_even - t_low, forward(t_low, 1, LANES), state)
-        peak, mass = lax.fori_loop(0, twos, forward(t_even, 2, LANES), state)
+        for start, stop, lanes in spans:
+            odd = lax.rem(stop - start, 2)
+            state = lax.fori_loop(0, odd, forward(start, 1, lanes), state)
+            state = lax.fori_loop(0, (stop - start) // 2, forward(start + odd, 2, lanes), state)
+        peak, mass = state
 
         tops = [[peak[:, i * WIDTH:(i + 1) * WIDTH]] for i in range(SPAN)]
         for e in range(SPAN):
@@ -461,25 +461,22 @@
             dv_acc[first + e] = grad_v
             dk_acc[first + e] = grad_k
 
-        def backward(stop, held):
-            def step(t, carried):
-                grad_v, grad_k = pull(t, 0, stop, held)
-                dv_acc[t] += grad_v
-                dk_acc[t] += grad_k
+        def backward(base, width, stop):
+            def step(n, carried):
+                for i in range(width):
+                    t = base + n * width + i
+                    grad_v, grad_k = pull(t, 0, stop, stop < LANES or width == 2)
+                    dv_acc[t] += grad_v
+                    dk_acc[t] += grad_k
                 return carried
 
             return step
 
-        lax.fori_loop(t_one, t_two, backward(WIDTH, True), 0)
-        lax.fori_loop(t_two, t_low, backward(2 * WIDTH, True), 0)
-        lax.fori_loop(t_low, t_even, backward(LANES, False), 0)
-
-        def backward_two(n, carried):
-            for i in range(2):
-                backward(LANES, True)(t_even + n * 2 + i, carried)
-            return carried
-
-        lax.fori_loop(0, twos, backward_two, 0)
+        for start, stop, lanes in spans:
+            odd = lax.rem(stop - start, 2) if lanes == LANES else stop - start
+            lax.fori_loop(0, odd, backward(start, 1, lanes), 0)
+            if lanes == LANES:
+                lax.fori_loop(0, (stop - start) // 2, backward(start + odd, 2, lanes), 0)
         grad = dqt_acc[...].T * SCALE
         for i in range(SPAN):
             for m in range(GROUP):

time: 75.2 us -> 71.6 us (0.952)
  Pallas kernels: 74 us -> 70.8 us
    pallas_call x1, Pallas kernels: 17.1 us -> 13.9 us  [attention(): pl.pallas_call(attention_kernel, name='attention', out_shape=(jax.ShapeDt...]
where the time goes in v7:
time: 71.6 us; the launch traced here: 71.5 us
  Pallas kernels  70.8 us (99%)
    pallas_call x1, Pallas kernels, exchange(): pl.pallas_call(exchange_kernel, name='exchange', out_shape=(jax.ShapeDtyp...  40.1 us
    pallas_call x1, Pallas kernels, reduce(): pl.pallas_call(reduce_kernel, name='reduce', out_shape=(jax.ShapeDtypeStr...  15 us
    pallas_call x1, Pallas kernels, attention(): pl.pallas_call(attention_kernel, name='attention', out_shape=(jax.ShapeDt...  13.9 us
    pallas_call x1, Pallas kernels, finish(): pl.pallas_call(finish_kernel, name='finish', out_shape=(out, out), in_spe...  1.81 us

profile of v7, /device:TPU:1, one launch (start us, length us, event | category | flops | bytes accessed | tf_op | source)
XLA Modules:
  0.0 71.5 jit_solution(5539207404962142114)
XLA Ops:
  0.6 40.1 %exchange.1 = (bf16[16,16,1024]{2,1,0:T(8,128)(2,1)}, bf16[16,16,1024]{2,1,0:T(8,128)(2,1)}, bf16[4096,128]{1,0:T(8,128)(2,1)}, bf16[4096,128]{1,0:T(8,128)(2,1)...) custom-call(s32[16,16]{1,0:T(8,128)} %route_hbm.3, bf16[2,16,8192]{2,1,0:T(8,128)(2,1)} %bitcast.10, ...), custom_call_target="tpu_custom_call" | custom-call | tf_op jit(solution)/shard_map/exchange/pallas_call | solution.py:255
  40.7 13.9 %attention.1 = (bf16[16,16,1024]{2,1,0:T(8,128)(2,1)}, f32[16,16,1024]{2,1,0:T(8,128)}, bf16[16,16,2,16,128]{4,3,2,1,0:T(8,128)(2,1)}) custom-call(s32[16,16]{1,0:T(8,128)} %route_hbm.3, s32[8]{0:T(128)} %docs_hbm.1, bf16[16,16,1024]{2,1,0:T(8,128)(2,1)} %get-tuple-element.17.q_hbm, bf16[16,16,1024]{2,1,0:T(8,128)(2,1)} %get-tuple-element.18.g_hbm, ...), custom_call_target="tpu_custom_call" | custom-call | tf_op jit(solution)/shard_map/attention/pallas_call | solution.py:512
  54.7 15.0 %reduce.1 = (bf16[4,16,16,128]{3,2,1,0:T(8,128)(2,1)}, f32[2,16,16,128]{3,2,1,0:T(8,128)}) custom-call(bf16[16,16,2,16,128]{4,3,2,1,0:T(8,128)(2,1)} %get-tuple-element.25.part), custom_call_target="tpu_custom_call" | custom-call | tf_op jit(solution)/shard_map/reduce/pallas_call | solution.py:640
  69.6 1.8 %finish.1 = (f32[16,16,128]{2,1,0:T(8,128)}, f32[16,16,128]{2,1,0:T(8,128)}) custom-call(bf16[4,16,16,128]{3,2,1,0:T(8,128)(2,1)} %get-tuple-element.26.chip_hbm, f32[2,16,16,128]{3,2,1,0:T(8,128)} %get-tuple-element.27.keep_hbm), custom_call_target="tpu_custom_call" | custom-call | tf_op jit(solution)/shard_map/finish/pallas_call | solution.py:697

commit v8 on v7

--- a/solution.py
+++ b/solution.py
@@ -554,7 +554,7 @@
     other = ctx_of(x, yl, core + 1)
     across = ctx_of(x, yl + 1, core)
     far = (2, 1, 3, 0)
-    order = [(dx, dy) for dx in far for dy in (1, 0)]
+    order = [(dx, dy) for dy in (1, 0) for dx in far]
 
     def along(dx):
         return ctx_of(x + dx, yl, core)

time: 71.6 us -> 70.1 us (0.979)
  Pallas kernels: 70.8 us -> 69.3 us
    pallas_call x1, Pallas kernels: 13.9 us -> 12.5 us  [attention(): pl.pallas_call(attention_kernel, name='attention', out_shape=(jax.ShapeDt...]
where the time goes in v8:
time: 70.1 us; the launch traced here: 69.9 us
  Pallas kernels  69.3 us (99%)
    pallas_call x1, Pallas kernels, exchange(): pl.pallas_call(exchange_kernel, name='exchange', out_shape=(jax.ShapeDtyp...  40.1 us
    pallas_call x1, Pallas kernels, reduce(): pl.pallas_call(reduce_kernel, name='reduce', out_shape=(jax.ShapeDtypeStr...  14.8 us
    pallas_call x1, Pallas kernels, attention(): pl.pallas_call(attention_kernel, name='attention', out_shape=(jax.ShapeDt...  12.5 us
    pallas_call x1, Pallas kernels, finish(): pl.pallas_call(finish_kernel, name='finish', out_shape=(out, out), in_spe...  1.81 us

profile of v8, /device:TPU:1, one launch (start us, length us, event | category | flops | bytes accessed | tf_op | source)
XLA Modules:
  0.0 69.9 jit_solution(2553767585789546)
XLA Ops:
  0.6 40.1 %exchange.1 = (bf16[16,16,1024]{2,1,0:T(8,128)(2,1)}, bf16[16,16,1024]{2,1,0:T(8,128)(2,1)}, bf16[4096,128]{1,0:T(8,128)(2,1)}, bf16[4096,128]{1,0:T(8,128)(2,1)...) custom-call(s32[16,16]{1,0:T(8,128)} %route_hbm.3, bf16[2,16,8192]{2,1,0:T(8,128)(2,1)} %bitcast.10, ...), custom_call_target="tpu_custom_call" | custom-call | tf_op jit(solution)/shard_map/exchange/pallas_call | solution.py:255
  40.7 12.5 %attention.1 = (bf16[16,16,1024]{2,1,0:T(8,128)(2,1)}, f32[16,16,1024]{2,1,0:T(8,128)}, bf16[16,16,2,16,128]{4,3,2,1,0:T(8,128)(2,1)}) custom-call(s32[16,16]{1,0:T(8,128)} %route_hbm.3, s32[8]{0:T(128)} %docs_hbm.1, bf16[16,16,1024]{2,1,0:T(8,128)(2,1)} %get-tuple-element.17.q_hbm, bf16[16,16,1024]{2,1,0:T(8,128)(2,1)} %get-tuple-element.18.g_hbm, ...), custom_call_target="tpu_custom_call" | custom-call | tf_op jit(solution)/shard_map/attention/pallas_call | solution.py:512
  53.3 14.8 %reduce.1 = (bf16[4,16,16,128]{3,2,1,0:T(8,128)(2,1)}, f32[2,16,16,128]{3,2,1,0:T(8,128)}) custom-call(bf16[16,16,2,16,128]{4,3,2,1,0:T(8,128)(2,1)} %get-tuple-element.25.part), custom_call_target="tpu_custom_call" | custom-call | tf_op jit(solution)/shard_map/reduce/pallas_call | solution.py:640
  68.1 1.8 %finish.1 = (f32[16,16,128]{2,1,0:T(8,128)}, f32[16,16,128]{2,1,0:T(8,128)}) custom-call(bf16[4,16,16,128]{3,2,1,0:T(8,128)(2,1)} %get-tuple-element.26.chip_hbm, f32[2,16,16,128]{3,2,1,0:T(8,128)} %get-tuple-element.27.keep_hbm), custom_call_target="tpu_custom_call" | custom-call | tf_op jit(solution)/shard_map/finish/pallas_call | solution.py:697

commit v9 on v8

--- a/solution.py
+++ b/solution.py
@@ -347,7 +347,7 @@
 
     def group(n, carry):
         first = n * SPAN
-        for copy in incoming(n):
+        for copy in incoming(n)[:4]:
             copy.wait()
         qg = stack(q, first)
         gg = stack(g, first)
@@ -417,6 +417,8 @@
             state = lax.fori_loop(0, (stop - start) // 2, forward(start + odd, 2, lanes), state)
         peak, mass = state
 
+        for copy in incoming(n)[4:]:
+            copy.wait()
         tops = [[peak[:, i * WIDTH:(i + 1) * WIDTH]] for i in range(SPAN)]
         for e in range(SPAN):
             s = masked(first + e, e * WIDTH)

time: 70.1 us -> 71.8 us (1.024)
  Pallas kernels: 69.3 us -> 71.3 us
    pallas_call x1, Pallas kernels: 12.5 us -> 15.6 us  [attention(): pl.pallas_call(attention_kernel, name='attention', out_shape=(jax.ShapeDt...]
    pallas_call x1, Pallas kernels: 14.8 us -> 13.7 us  [reduce(): pl.pallas_call(reduce_kernel, name='reduce', out_shape=(jax.ShapeDtypeStr...]
where the time goes in v9:
time: 71.8 us; the launch traced here: 71.9 us
  Pallas kernels  71.3 us (99%)
    pallas_call x1, Pallas kernels, exchange(): pl.pallas_call(exchange_kernel, name='exchange', out_shape=(jax.ShapeDtyp...  40.1 us
    pallas_call x1, Pallas kernels, attention(): pl.pallas_call(attention_kernel, name='attention', out_shape=(jax.ShapeDt...  15.6 us
    pallas_call x1, Pallas kernels, reduce(): pl.pallas_call(reduce_kernel, name='reduce', out_shape=(jax.ShapeDtypeStr...  13.7 us
    pallas_call x1, Pallas kernels, finish(): pl.pallas_call(finish_kernel, name='finish', out_shape=(out, out), in_spe...  1.81 us

profile of v9, /device:TPU:1, one launch (start us, length us, event | category | flops | bytes accessed | tf_op | source)
XLA Modules:
  0.0 71.9 jit_solution(11314043295212679387)
XLA Ops:
  0.6 40.1 %exchange.1 = (bf16[16,16,1024]{2,1,0:T(8,128)(2,1)}, bf16[16,16,1024]{2,1,0:T(8,128)(2,1)}, bf16[4096,128]{1,0:T(8,128)(2,1)}, bf16[4096,128]{1,0:T(8,128)(2,1)...) custom-call(s32[16,16]{1,0:T(8,128)} %route_hbm.3, bf16[2,16,8192]{2,1,0:T(8,128)(2,1)} %bitcast.10, ...), custom_call_target="tpu_custom_call" | custom-call | tf_op jit(solution)/shard_map/exchange/pallas_call | solution.py:255
  40.7 15.6 %attention.1 = (bf16[16,16,1024]{2,1,0:T(8,128)(2,1)}, f32[16,16,1024]{2,1,0:T(8,128)}, bf16[16,16,2,16,128]{4,3,2,1,0:T(8,128)(2,1)}) custom-call(s32[16,16]{1,0:T(8,128)} %route_hbm.3, s32[8]{0:T(128)} %docs_hbm.1, bf16[16,16,1024]{2,1,0:T(8,128)(2,1)} %get-tuple-element.17.q_hbm, bf16[16,16,1024]{2,1,0:T(8,128)(2,1)} %get-tuple-element.18.g_hbm, ...), custom_call_target="tpu_custom_call" | custom-call | tf_op jit(solution)/shard_map/attention/pallas_call | solution.py:514
  56.4 13.7 %reduce.1 = (bf16[4,16,16,128]{3,2,1,0:T(8,128)(2,1)}, f32[2,16,16,128]{3,2,1,0:T(8,128)}) custom-call(bf16[16,16,2,16,128]{4,3,2,1,0:T(8,128)(2,1)} %get-tuple-element.25.part), custom_call_target="tpu_custom_call" | custom-call | tf_op jit(solution)/shard_map/reduce/pallas_call | solution.py:642
  70.1 1.8 %finish.1 = (f32[16,16,128]{2,1,0:T(8,128)}, f32[16,16,128]{2,1,0:T(8,128)}) custom-call(bf16[4,16,16,128]{3,2,1,0:T(8,128)(2,1)} %get-tuple-element.26.chip_hbm, f32[2,16,16,128]{3,2,1,0:T(8,128)} %get-tuple-element.27.keep_hbm), custom_call_target="tpu_custom_call" | custom-call | tf_op jit(solution)/shard_map/finish/pallas_call | solution.py:699
